TPU v7x, 128 devices: a whole 4x4x4 slice. The times are simulated.
128 devices in a mesh: group: 8 (over y, core), inner: 16 (over x, z).
Axes of the slice: x: 4, y: 4, z: 4, core: 2. Of those that a mesh axis runs over, the one named last changes fastest.
Arguments:
- grad_out: bfloat16 [16384, 2048], P(('group', 'inner')), may hold values from -4 to 4
- hidden_in: bfloat16 [16384, 2048], P(('group', 'inner')), may hold values from -6 to 6
- norm_gain: float32 [2048], replicated, may hold values from 0.5 to 1.5
- expert_ids: int32 [16384, 8], P(('group', 'inner')), may hold values from 0 to 127, all different within a row; in each aligned block of 128 rows (0 to 127, 128 to 255, ...) at most 10 rows name the same one
- gate_weights: float32 [16384, 8], P(('group', 'inner')), may hold values from 0.02 to 0.5
- gate_proj: bfloat16 [128, 2048, 768], P(('group', 'inner')), may hold values from -0.125 to 0.125
- up_proj: bfloat16 [128, 2048, 768], P(('group', 'inner')), may hold values from -0.125 to 0.125
- down_proj: bfloat16 [128, 768, 2048], P(('group', 'inner')), may hold values from -0.21875 to 0.21875
- out_proj: bfloat16 [4096, 2048], P('inner'), may hold values from -0.09375 to 0.09375
- query_rows: bfloat16 [16384, 4096], P('group', 'inner'), may hold values from -140 to 140
- key_rows: bfloat16 [16384, 4096], P('group', 'inner'), may hold values from -7 to 7
- value_rows: bfloat16 [16384, 4096], P('group', 'inner'), may hold values from -6 to 6
Outputs:
- grad_hidden: bfloat16 [16384, 2048], P(('group', 'inner'))
- grad_gate: bfloat16 [16384, 8], P(('group', 'inner'))
- grad_queries: bfloat16 [16384, 4096], P('group', 'inner')
- grad_keys: bfloat16 [16384, 4096], P('group', 'inner')
- grad_values: bfloat16 [16384, 4096], P('group', 'inner')
Inputs may be any that keep to these rules, and one draw needn't show every extreme that they name: `expert_ids`: each row names 8 different experts; in the rows of one device no expert is named more than 10 times, a bound that some block reaches.
All inputs are finite; a program needn't handle non-finite values.
Results may differ from a plain program's by a relative error of at most 0.019.
Values may be sent and summed in bfloat16 or wider, within the bound.
No kernel may reach another device: no remote copies, remote signals or barrier semaphores. Data moves between devices by JAX's collectives and lax.ppermute only.
A program may use at most 128 MiB of HBM per device.

v0:
```python
import jax
import jax.numpy as jnp
from jax import lax
from jax.sharding import PartitionSpec as P

HD = 128
SEQS = 2


def dot_rt(left, right):
    return lax.dot_general(
        left, right, (((1,), (1,)), ((), ())), preferred_element_type=jnp.float32
    )


def dot_lt(left, right):
    return lax.dot_general(
        left, right, (((0,), (0,)), ((), ())), preferred_element_type=jnp.float32
    )


def expert_backward(arrived, gate_mat, up_mat, down_mat):
    model_width = gate_mat.shape[0]
    grad_in = arrived[:, :model_width]
    normed_in = arrived[:, model_width:]
    gate_pre = jnp.dot(normed_in, gate_mat, preferred_element_type=jnp.float32)
    up_pre = jnp.dot(normed_in, up_mat, preferred_element_type=jnp.float32)
    sigma = jax.nn.sigmoid(gate_pre)
    act = gate_pre * sigma
    slope = sigma * (1.0 + gate_pre * (1.0 - sigma))
    expert_hidden = act * up_pre
    grad_hid = dot_rt(grad_in, down_mat)
    gate_score = jnp.sum(grad_hid * expert_hidden, axis=1).astype(jnp.bfloat16)
    grad_gatepre = (grad_hid * up_pre * slope).astype(jnp.bfloat16)
    grad_uppre = (grad_hid * act).astype(jnp.bfloat16)
    pair_grad = (dot_rt(grad_gatepre, gate_mat) + dot_rt(grad_uppre, up_mat)).astype(jnp.bfloat16)
    return (pair_grad, gate_score)


def local(
    grad_out,
    hidden_in,
    norm_gain,
    expert_ids,
    gate_weights,
    gate_proj,
    up_proj,
    down_proj,
    out_proj,
    query_rows,
    key_rows,
    value_rows,
):
    tok_dev, model_width = grad_out.shape
    top_count = expert_ids.shape[1]
    groups = lax.axis_size("group")
    inner_size = lax.axis_size("inner")
    experts = groups * inner_size
    capacity = max(2, 5 * tok_dev * top_count // (4 * experts))
    local_heads = out_proj.shape[0] // HD
    length = query_rows.shape[0] // SEQS
    att_scale = HD ** (-0.5)
    causal = jnp.arange(length)[:, None] >= jnp.arange(length)[None, :]

    def by_head(matrix):
        return (
            matrix.reshape(SEQS, length, local_heads, HD)
            .transpose(0, 2, 1, 3)
            .reshape(SEQS * local_heads, length, HD)
        )

    def by_token(stacked):
        return (
            stacked.reshape(SEQS, local_heads, length, HD)
            .transpose(0, 2, 1, 3)
            .reshape(SEQS * length, local_heads * HD)
        )

    def masked_scores(query, key_part):
        return jnp.where(causal, dot_rt(query, key_part) * att_scale, -jnp.inf)

    query_items = by_head(query_rows)
    key_items = by_head(key_rows)
    value_items = by_head(value_rows)
    hid_full = hidden_in.astype(jnp.float32)
    inv_rms = lax.rsqrt(jnp.mean(hid_full * hid_full, axis=1, keepdims=True) + 1e-06)
    normal_rows = hid_full * inv_rms
    normed = (normal_rows * norm_gain).astype(jnp.bfloat16)
    flat_ids = expert_ids.reshape(-1)
    pair_count = flat_ids.shape[0]
    onehot = (flat_ids[:, None] == jnp.arange(experts, dtype=jnp.int32)[None, :]).astype(jnp.int32)
    earlier = jnp.cumsum(onehot, axis=0) - onehot
    slot_index = jnp.sum(earlier * onehot, axis=1)
    target = flat_ids * capacity + slot_index
    token_rows = jnp.concatenate([grad_out, normed], axis=1)
    blank_row = jnp.zeros((1, 2 * model_width), jnp.bfloat16)
    owner_token = (
        jnp.full((experts * capacity,), tok_dev, jnp.int32)
        .at[target]
        .set(jnp.arange(pair_count, dtype=jnp.int32) // top_count)
    )
    send_rows = jnp.concatenate([token_rows, blank_row], axis=0)
    outgoing = send_rows[owner_token]
    arrived = lax.all_to_all(
        outgoing.reshape(experts, capacity, 2 * model_width),
        ("group", "inner"),
        split_axis=0,
        concat_axis=0,
        tiled=True,
    )
    arrived = arrived.reshape(experts * capacity, 2 * model_width)
    pair_grad, gate_score = expert_backward(arrived, gate_proj[0], up_proj[0], down_proj[0])
    returned, score_back = (
        lax.all_to_all(
            pair_grad.reshape(experts, capacity, model_width),
            ("group", "inner"),
            split_axis=0,
            concat_axis=0,
            tiled=True,
        ),
        lax.all_to_all(
            gate_score.reshape(experts, capacity),
            ("group", "inner"),
            split_axis=0,
            concat_axis=0,
            tiled=True,
        ),
    )
    returned = returned.reshape(experts * capacity, model_width)[target]
    grad_gate = score_back.reshape(experts * capacity)[target].reshape(tok_dev, top_count)
    moe_grad = jnp.einsum(
        "tk,tkd->td",
        gate_weights,
        returned.reshape(tok_dev, top_count, model_width).astype(jnp.float32),
    )
    scaled = moe_grad * norm_gain
    inner_mean = jnp.mean(scaled * normal_rows, axis=1, keepdims=True)
    grad_hidden = (
        grad_out.astype(jnp.float32) + inv_rms * (scaled - normal_rows * inner_mean)
    ).astype(jnp.bfloat16)
    grad_attn = dot_rt(lax.all_gather(grad_hidden, "inner", axis=0, tiled=True), out_proj).astype(
        jnp.bfloat16
    )
    grad_items = by_head(grad_attn)

    def attend(block_item):
        query, key_part, value, grad_part = block_item
        scores = masked_scores(query, key_part)
        peak = jnp.max(scores, axis=1, keepdims=True)
        exp_scores = jnp.exp(scores - peak)
        probs = exp_scores / jnp.sum(exp_scores, axis=1, keepdims=True)
        probs_half = probs.astype(jnp.bfloat16)
        grad_v = dot_lt(probs_half, grad_part).astype(jnp.bfloat16)
        grad_probs = dot_rt(grad_part, value)
        delta = jnp.sum(probs * grad_probs, axis=1, keepdims=True)
        grad_scores = (probs * (grad_probs - delta)).astype(jnp.bfloat16)
        grad_q = (
            att_scale * jnp.dot(grad_scores, key_part, preferred_element_type=jnp.float32)
        ).astype(jnp.bfloat16)
        grad_k = (att_scale * dot_lt(grad_scores, query)).astype(jnp.bfloat16)
        return (grad_q, grad_k, grad_v)

    results = lax.map(
        lambda block_item: attend(block_item), (query_items, key_items, value_items, grad_items)
    )
    return (
        grad_hidden,
        grad_gate,
        by_token(results[0]),
        by_token(results[1]),
        by_token(results[2]),
    )


def solution(mesh):
    in_specs = (
        P(("group", "inner"), None),
        P(("group", "inner"), None),
        P(),
        P(("group", "inner"), None),
        P(("group", "inner"), None),
        P(("group", "inner"), None, None),
        P(("group", "inner"), None, None),
        P(("group", "inner"), None, None),
        P("inner", None),
        P("group", "inner"),
        P("group", "inner"),
        P("group", "inner"),
    )
    out_specs = (
        P(("group", "inner"), None),
        P(("group", "inner"), None),
        P("group", "inner"),
        P("group", "inner"),
        P("group", "inner"),
    )
    return jax.shard_map(local, mesh=mesh, in_specs=in_specs, out_specs=out_specs, check_vma=False)
```

profile of v0, /device:TPU:0, one launch (start us, length us, event | category | flops | bytes accessed | tf_op | source)
XLA Modules:
  0.0 606.7 jit_solution(12722173982319907187)
XLA Ops:
  13.7 4.3 scatter_custom_fusion
  22.7 20.2 %gather_fusion = bf16[1280,4096]{1,0:T(8,128)(2,1)} fusion(bf16[129,4096]{1,0:T(8,128)(2,1)} %fusion.65, s32[2048]{0:T(1024)S(1)} %pad_clamp_fusion), kind=kCustom, calls=%fused_computation | custom fusion | bytes 20976640 | tf_op jit(solution)/shard_map/gather | solution.py:103
  42.9 15.2 %reshape.152 = bf16[128,10,4096]{2,1,0:T(8,128)(2,1)} reshape(bf16[1280,4096]{1,0:T(8,128)(2,1)} %gather_fusion) | data formatting | bytes 20971520 | tf_op jit(solution)/shard_map/reshape | solution.py:105
  58.1 200.3 %all_to_all.16 = bf16[128,10,4096]{2,1,0:T(8,128)(2,1)} all-to-all(bf16[128,10,4096]{2,1,0:T(8,128)(2,1)} %reshape.152), channel_id=1, replica_groups=mesh['group'=8,'inner'=16] {'group','inner'}, dimensions={0} | all-to-all | bytes 20971520 | tf_op jit(solution)/shard_map/all_to_all | solution.py:104
  258.3 16.5 %reshape.153 = bf16[1280,4096]{1,0:T(8,128)(2,1)} reshape(bf16[128,10,4096]{2,1,0:T(8,128)(2,1)} %all_to_all.16) | data formatting | bytes 20971520 | tf_op jit(solution)/shard_map/reshape | solution.py:111
  274.9 7.3 %fusion.46 = f32[1280,768]{0,1:T(8,128)S(1)} fusion(bf16[1280,4096]{1,0:T(8,128)(2,1)} %reshape.153, bf16[1,2048,768]{2,1,0:T(8,128)(2,1)S(1)} %copy-done), kind=kOutput, calls=%fused_computation.50 | convolution fusion | flops 4026531840 | bytes 12320768 | tf_op jit(solution)/shard_map/dot_general | solution.py:26
  282.3 6.3 %fusion.48 = f32[1280,768]{0,1:T(8,128)} fusion(bf16[1280,4096]{1,0:T(8,128)(2,1)S(1)} %copy-done.2, bf16[1,2048,768]{2,1,0:T(8,128)(2,1)S(1)} %copy-done.11), kind=kOutput, calls=%fused_computation.52 | convolution fusion | flops 4026531840 | bytes 12320768 | tf_op jit(solution)/shard_map/dot_general | solution.py:27
  288.5 7.7 %multiply_reduce_fusion.1 = (bf16[1280]{0:T(1024)(128)(2,1)S(1)}, f32[1280,768]{0,1:T(8,128)}) fusion(f32[1280,768]{0,1:T(8,128)} %fusion.48, f32[1280,768]{0,1:T(8,128)S(1)} %fusion.46, bf16[1,768,2048]{2,1,0:T(8,128)(2,1)S(1)} %copy-done.10, bf16[1280,4096]{1,0:T(8,128)(2,1)S(1)} %copy-done.2), kind=kOutput, calls=%fused_computation.56 | convolution fusion | flops 4033411840 | bytes 20187648 | tf_op jit(solution)/shard_map/dot_general | solution.py:11
  296.2 12.7 %fusion.53 = f32[1280,2048]{1,0:T(8,128)} fusion(bf16[1,2048,768]{2,1,0:T(8,128)(2,1)S(1)} %copy-done, f32[1280,768]{0,1:T(8,128)S(1)} %fusion.46, f32[1280,768]{0,1:T(8,128)} %get-tuple-element.106, f32[1280,768]{0,1:T(8,128)} %fusion.48), kind=kOutput, calls=%fused_computation.61 | convolution fusion | flops 4036362240 | bytes 25427968 | tf_op jit(solution)/shard_map/dot_general | solution.py:11
  308.9 10.4 %add_convert_fusion = bf16[1280,2048]{1,0:T(8,128)(2,1)} fusion(f32[1280,2048]{1,0:T(8,128)} %fusion.53, bf16[1,2048,768]{2,1,0:T(8,128)(2,1)S(1)} %copy-done.11, f32[1280,768]{0,1:T(8,128)} %get-tuple-element.106, f32[1280,768]{0,1:T(8,128)S(1)} %fusion.46), kind=kOutput, calls=%fused_computation.47 | convolution fusion | flops 4037672960 | bytes 26738688 | tf_op jit(solution)/shard_map/dot_general | solution.py:11
  319.3 9.5 %reshape.154 = bf16[128,10,2048]{2,1,0:T(8,128)(2,1)} reshape(bf16[1280,2048]{1,0:T(8,128)(2,1)} %add_convert_fusion) | data formatting | bytes 10485760 | tf_op jit(solution)/shard_map/reshape | solution.py:115
  328.8 7.2 %all-to-all-start.1 = ((bf16[128,10,2048]{2,1,0:T(8,128)(2,1)}), bf16[128,10,2048]{2,1,0:T(8,128)(2,1)}, u32[]{:S(2)}, u32[]{:S(2)}) async-start(bf16[128,10,2048]{2,1,0:T(8,128)(2,1)} %reshape.154), calls=%async_computation.1 | async-start | bytes 16777216 | tf_op jit(solution)/shard_map/all_to_all | solution.py:114
  336.3 100.3 %all-to-all-done.1 = bf16[128,10,2048]{2,1,0:T(8,128)(2,1)} async-done(((bf16[128,10,2048]{2,1,0:T(8,128)(2,1)}), bf16[128,10,2048]{2,1,0:T(8,128)(2,1)}, u32[]{:S(2)}, u32[]{:S(2)}) %all-to-all-start.1) | async-done | bytes 5242912 | tf_op jit(solution)/shard_map/all_to_all | solution.py:114
  436.6 9.8 %reshape.155 = bf16[1280,2048]{1,0:T(8,128)(2,1)} reshape(bf16[128,10,2048]{2,1,0:T(8,128)(2,1)} %all-to-all-done.1) | data formatting | bytes 10485760 | tf_op jit(solution)/shard_map/reshape | solution.py:129
  446.4 12.0 %gather_fusion.1 = bf16[1024,2048]{1,0:T(8,128)(2,1)} fusion(bf16[1280,2048]{1,0:T(8,128)(2,1)} %reshape.155, s32[1024]{0:T(1024)S(1)} %broadcast_clamp_fusion), kind=kCustom, calls=%fused_computation.1 | custom fusion | bytes 8392704 | tf_op jit(solution)/shard_map/gather | solution.py:129
  458.4 3.6 fusion.50
  464.7 10.3 %all-to-all-start.2 = ((bf16[128,1,10]{2,1,0:T(2,128)(2,1)}), bf16[128,1,10]{2,1,0:T(2,128)(2,1)S(1)}, u32[]{:S(2)}, u32[]{:S(2)}) async-start(bf16[128,1,10]{2,1,0:T(2,128)(2,1)} %convert_element_type.78), calls=%async_computation.2 | async-start | bytes 131072 | tf_op jit(solution)/shard_map/all_to_all | solution.py:121
  479.5 5.1 all-to-all-done.2
  484.9 6.8 %gather_fusion.2 = bf16[1024]{0:T(1024)(128)(2,1)S(1)} fusion(bf16[1280]{0:T(1024)(128)(2,1)S(1)} %reshape.157, s32[1024]{0:T(1024)S(1)} %broadcast_clamp_fusion), kind=kCustom, calls=%fused_computation.2 | custom fusion | bytes 8192 | tf_op jit(solution)/shard_map/gather | solution.py:130
  492.5 44.0 %all-gather.2.cloned.1.call-done = bf16[2048,2048]{1,0:T(8,128)(2,1)} async-done(((bf16[128,2048]{1,0:T(8,128)(2,1)}), bf16[2048,2048]{1,0:T(8,128)(2,1)}) %all-gather.2.cloned.1.call-update) | async-done | bytes 8388624 | tf_op jit(solution)/shard_map/all_gather | solution.py:141
  536.6 6.0 convolution_convert_fusion
  544.0 45.7 %while.15 = (s32[]{:T(128)}, bf16[4,1024,128]{2,1,0:T(8,128)(2,1)}, bf16[4,1024,128]{2,1,0:T(8,128)(2,1)}, bf16[4,1024,128]{2,1,0:T(8,128)(2,1)}, bf16[4,1024,12...) while((s32[]{:T(128)}, bf16[4,1024,128]{2,1,0:T(8,128)(2,1)}, ...), condition=%wide.region_11.12_spmd.clone, body=%wide.region_7.11_spmd.clone.sunk | while | flops 1374286848 | bytes 38323292 | solution.py:163
  546.2 2.4 fusion.112
  552.9 2.4 fusion.110
  557.5 2.4 fusion.112
  564.3 2.4 fusion.110
  568.9 2.4 fusion.112
  575.6 2.4 fusion.110
  580.2 2.4 fusion.112
  587.0 2.4 fusion.110
  589.6 2.3 copy.48
  594.3 2.5 copy.47
  (92 shorter events, 52.2 us)
Async XLA Ops:
  7.2 267.7 %copy-start = (bf16[1,2048,768]{2,1,0:T(8,128)(2,1)S(1)}, bf16[1,2048,768]{2,1,0:T(8,128)(2,1)}, u32[]{:S(2)}) copy-start(bf16[1,2048,768]{2,1,0:T(8,128)(2,1)} %param.19) | copy-start | bytes 9437188
  7.2 12.2 %copy-start.8 = (f32[2048]{0:T(1024)S(1)}, f32[2048]{0:T(1024)}, u32[]{:S(2)}) copy-start(f32[2048]{0:T(1024)} %param.16) | copy-start | bytes 24580
  9.3 0.8 copy-start.4
  274.9 7.4 %copy-start.2 = (bf16[1280,4096]{1,0:T(8,128)(2,1)S(1)}, bf16[1280,4096]{1,0:T(8,128)(2,1)}, u32[]{:S(2)}) copy-start(bf16[1280,4096]{1,0:T(8,128)(2,1)} %reshape.153) | copy-start | bytes 31457284
  274.9 7.4 %copy-start.11 = (bf16[1,2048,768]{2,1,0:T(8,128)(2,1)S(1)}, bf16[1,2048,768]{2,1,0:T(8,128)(2,1)}, u32[]{:S(2)}) copy-start(bf16[1,2048,768]{2,1,0:T(8,128)(2,1)} %param.20) | copy-start | bytes 9437188
  282.2 6.3 %copy-start.10 = (bf16[1,768,2048]{2,1,0:T(8,128)(2,1)S(1)}, bf16[1,768,2048]{2,1,0:T(8,128)(2,1)}, u32[]{:S(2)}) copy-start(bf16[1,768,2048]{2,1,0:T(8,128)(2,1)} %param.21) | copy-start | bytes 9437188
  328.8 7.3 %copy-start.9 = (f32[128,8]{0,1:T(8,128)S(1)}, f32[128,8]{0,1:T(8,128)}, u32[]{:S(2)}) copy-start(f32[128,8]{0,1:T(8,128)} %param.18) | copy-start | bytes 12292
  328.8 107.8 %all-to-all-start.1 = ((bf16[128,10,2048]{2,1,0:T(8,128)(2,1)}), bf16[128,10,2048]{2,1,0:T(8,128)(2,1)}, u32[]{:S(2)}, u32[]{:S(2)}) async-start(bf16[128,10,2048]{2,1,0:T(8,128)(2,1)} %reshape.154), calls=%async_computation.1 | async-start | bytes 16777216 | tf_op jit(solution)/shard_map/all_to_all | solution.py:114
  336.1 200.5 %all-gather.2.cloned.1.call-start = ((), (), s32[]{:S(2)}) async-start(), calls=%async_computation.3 | async-start | bytes 8912896 | tf_op jit(solution)/shard_map/all_gather | solution.py:141
  458.4 3.6 copy-start.3
  458.4 4.0 copy-start.5
  458.4 16.6 %copy-start.6 = (bf16[2048,256]{1,0:T(8,128)(2,1)S(1)}, bf16[2048,256]{1,0:T(8,128)(2,1)}, u32[]{:S(2)}) copy-start(bf16[2048,256]{1,0:T(8,128)(2,1)} %param.23) | copy-start | bytes 3145732
  464.7 19.9 %all-to-all-start.2 = ((bf16[128,1,10]{2,1,0:T(2,128)(2,1)}), bf16[128,1,10]{2,1,0:T(2,128)(2,1)S(1)}, u32[]{:S(2)}, u32[]{:S(2)}) async-start(bf16[128,1,10]{2,1,0:T(2,128)(2,1)} %convert_element_type.78), calls=%async_computation.2 | async-start | bytes 131072 | tf_op jit(solution)/shard_map/all_to_all | solution.py:121
  475.1 3.0 copy-start.7
  594.3 5.3 copy-start.1
Sparse Core Ops, SparseCore 0:
  464.0 72.4 all-gather.1
where the time goes:
time: 615 us; the launch traced here: 607 us
  blocking collectives  200 us (33%)
  waiting for transfers between devices  149 us (24%)
  local copies, waits for them, and re-layouts  115 us (19%)
  matrix products  93.2 us (15%)
  starting transfers between devices  17.6 us (3%)
  other arithmetic  16.2 us (3%)
  between operations  14.6 us (2%)
    all_to_all x1, blocking collectives, local(): lax.all_to_all(outgoing.reshape(experts, capacity, 2 * model_width), ('gr...  200 us
    all_to_all x1, waiting for transfers between devices, local(): lax.all_to_all(pair_grad.reshape(experts, capacity, model_width), ('group...  100 us
    dot_general x12, matrix products, dot_rt(): lax.dot_general(left, right, (((1,), (1,)), ((), ())), preferred_element_...  51 us
    all_gather x1, waiting for transfers between devices, local(): lax.all_gather(grad_hidden, 'inner', axis=0, tiled=True)  44 us
    gather x1, local copies, waits for them, and re-layouts, local(): outgoing = send_rows[owner_token]  20.2 us
    reshape x1, local copies, waits for them, and re-layouts, local(): arrived = arrived.reshape(experts * capacity, 2 * model_width)  16.5 us
    dot_general x8, matrix products, dot_lt(): lax.dot_general(left, right, (((0,), (0,)), ((), ())), preferred_element_...  15.3 us
    reshape x1, local copies, waits for them, and re-layouts, local(): outgoing.reshape(experts, capacity, 2 * model_width)  15.2 us
  transfers between devices with their start and end apart: 3, of which 3 were waited for; matrix products, arithmetic and copies ran while one was open for 2% of the time, Pallas kernels for 0%

commit v1 on v0

v1 whole, which is shorter than its diff:
```python
import functools

import jax
import jax.numpy as jnp
from jax import lax
from jax.experimental import pallas as pl
from jax.experimental.pallas import tpu as pltpu
from jax.sharding import PartitionSpec as P

HD = 128
SEQS = 2
SLOTS = 8
EXTRA = 2
PARTS = 4
LANES = 128
BF = jnp.bfloat16
F32 = jnp.float32


def dot_nn(left, right):
    return lax.dot_general(left, right, (((1,), (0,)), ((), ())), preferred_element_type=F32)


def dot_nt(left, right):
    return lax.dot_general(left, right, (((1,), (1,)), ((), ())), preferred_element_type=F32)


def dot_tn(left, right):
    return lax.dot_general(left, right, (((0,), (0,)), ((), ())), preferred_element_type=F32)


def iota(shape, dim):
    return lax.broadcasted_iota(jnp.int32, shape, dim)


def routing(ids, experts):
    tokens, top = ids.shape
    lane = iota((tokens, experts), 1)
    member = jnp.zeros((tokens, experts), F32)
    for k in range(top):
        member = member + jnp.where(ids[:, k : k + 1] == lane, 1.0, 0.0)
    earlier = jnp.where(iota((tokens, tokens), 1) < iota((tokens, tokens), 0), 1.0, 0.0).astype(BF)
    slot = dot_nn(earlier, member.astype(BF))
    return jnp.where(member > 0.5, slot, -1.0)


def per_row(by_expert):
    experts, width = by_expert.shape
    return jnp.broadcast_to(by_expert[:, None, :], (experts, SLOTS, width)).reshape(
        experts * SLOTS, width
    )


def dispatch_kernel(ids_ref, grad_ref, hid_ref, gain_ref, out_ref, rows_ref, parts_ref, slot_ref):
    tokens, width = grad_ref.shape
    experts = slot_ref.shape[0]
    step = pl.program_id(0)
    block_experts = out_ref.shape[0] // SLOTS
    piece = 2 * width // PARTS

    @pl.when(step == 0)
    def _():
        hid = hid_ref[...].astype(F32)
        inv_rms = lax.rsqrt(jnp.mean(hid * hid, axis=1, keepdims=True) + 1e-06)
        normed = (hid * inv_rms * gain_ref[...]).astype(BF)
        grad = grad_ref[...]
        rows_ref[:, :width] = grad
        rows_ref[:, width:] = normed
        half = PARTS // 2
        for part in range(half):
            parts_ref[part * tokens : (part + 1) * tokens, :] = grad[
                :, part * piece : (part + 1) * piece
            ]
            parts_ref[(half + part) * tokens : (half + part + 1) * tokens, :] = normed[
                :, part * piece : (part + 1) * piece
            ]
        slot_ref[...] = routing(ids_ref[...], experts).T

    start = pl.multiple_of(step * block_experts, block_experts)
    slot = per_row(slot_ref[pl.ds(start, block_experts), :])
    place = iota(slot.shape, 0) & (SLOTS - 1)
    pick = jnp.where(slot == place.astype(F32), 1.0, 0.0).astype(BF)
    chunk = 1024
    for col in range(0, 2 * width, chunk):
        out_ref[:, col : col + chunk] = dot_nn(pick, rows_ref[:, col : col + chunk]).astype(BF)
    late = slot == (SLOTS + (place >> 2)).astype(F32)
    pick_late = jnp.concatenate(
        [
            jnp.where(late & ((place & (PARTS - 1)) == part), 1.0, 0.0).astype(BF)
            for part in range(PARTS)
        ],
        axis=1,
    )
    out_ref[:, 2 * width :] = dot_nn(pick_late, parts_ref[...]).astype(BF)


def dispatch(ids, grad_out, hidden_in, gain, experts):
    tokens, width = grad_out.shape
    total = 2 * width + 2 * width // PARTS
    steps = 4
    rows = experts * SLOTS
    whole = lambda shape: pl.BlockSpec(shape, lambda i: (0,) * len(shape))
    return pl.pallas_call(
        dispatch_kernel,
        out_shape=jax.ShapeDtypeStruct((rows, total), BF),
        grid=(steps,),
        in_specs=[
            whole(ids.shape),
            whole(grad_out.shape),
            whole(hidden_in.shape),
            whole(gain.shape),
        ],
        out_specs=pl.BlockSpec((rows // steps, total), lambda i: (i, 0)),
        scratch_shapes=[
            pltpu.VMEM((tokens, 2 * width), BF),
            pltpu.VMEM((PARTS * tokens, 2 * width // PARTS), BF),
            pltpu.VMEM((experts, tokens), F32),
        ],
        compiler_params=pltpu.CompilerParams(vmem_limit_bytes=32 << 20),
        name="dispatch",
    )(ids, grad_out, hidden_in, gain)


def expert_kernel(rows_ref, gate_ref, up_ref, down_ref, out_ref, grad_ref, norm_ref):
    width = gate_ref.shape[0]
    main = rows_ref.shape[0]
    late = main // SLOTS * EXTRA
    half = width // 2
    grad_ref[:main, :] = rows_ref[:, :width]
    norm_ref[:main, :] = rows_ref[:, width : 2 * width]
    order = iota((main, main), 0)
    source = (order % late) * PARTS + order // late
    gather = jnp.where(iota((main, main), 1) == source, 1.0, 0.0).astype(BF)
    moved = dot_nn(gather, rows_ref[:, 2 * width :]).astype(BF)
    for part in range(2):
        cols = slice(part * half, (part + 1) * half)
        grad_ref[main:, cols] = moved[part * late : (part + 1) * late]
        norm_ref[main:, cols] = moved[(2 + part) * late : (3 + part) * late]
    norm = norm_ref[...]
    gate_pre = dot_nn(norm, gate_ref[...])
    up_pre = dot_nn(norm, up_ref[...])
    sigma = jax.nn.sigmoid(gate_pre)
    act = gate_pre * sigma
    slope = sigma * (1.0 + gate_pre * (1.0 - sigma))
    grad_hid = dot_nt(grad_ref[...], down_ref[...])
    grad_uppre = grad_hid * act
    score = jnp.sum(grad_uppre * up_pre, axis=1, keepdims=True)
    grad_gatepre = (grad_hid * up_pre * slope).astype(BF)
    grad_uppre = grad_uppre.astype(BF)
    pair = (dot_nt(grad_gatepre, gate_ref[...]) + dot_nt(grad_uppre, up_ref[...])).astype(BF)
    out_ref[:, :width] = pair[:main]
    quarter = width // PARTS
    stacked = jnp.concatenate(
        [pair[main:, part * quarter : (part + 1) * quarter] for part in range(PARTS)], axis=0
    )
    order = iota((main, main), 1)
    scatter = jnp.where(
        iota((main, main), 0) == (order % late) * PARTS + order // late, 1.0, 0.0
    ).astype(BF)
    out_ref[:, width : width + quarter] = dot_nn(scatter, stacked).astype(BF)
    spread = jnp.where((iota((main, late), 0) >> 2) == iota((main, late), 1), 1.0, 0.0).astype(BF)
    late_score = dot_nn(spread, jnp.broadcast_to(score[main:], (late, LANES)).astype(BF))
    lane = iota((main, LANES), 1)
    out_ref[:, width + quarter :] = jnp.where(
        lane == 0, score[:main], jnp.where(lane == 1, late_score, 0.0)
    ).astype(BF)


def expert_backward(arrived, gate_mat, up_mat, down_mat):
    rows, total = arrived.shape
    width, hidden = gate_mat.shape
    steps = 2
    main = rows // steps
    both = main + main // SLOTS * EXTRA
    out_width = width + width // PARTS + LANES
    fixed = lambda shape: pl.BlockSpec(
        shape, lambda i: (0,) * len(shape), pipeline_mode=pl.Buffered(1)
    )
    return pl.pallas_call(
        expert_kernel,
        out_shape=jax.ShapeDtypeStruct((rows, out_width), BF),
        grid=(steps,),
        in_specs=[
            pl.BlockSpec((main, total), lambda i: (i, 0)),
            fixed(gate_mat.shape),
            fixed(up_mat.shape),
            fixed(down_mat.shape),
        ],
        out_specs=pl.BlockSpec((main, out_width), lambda i: (i, 0)),
        scratch_shapes=[pltpu.VMEM((both, width), BF), pltpu.VMEM((both, width), BF)],
        compiler_params=pltpu.CompilerParams(vmem_limit_bytes=56 << 20),
        name="expert",
    )(arrived, gate_mat, up_mat, down_mat)


def combine_kernel(ids_ref, weight_ref, grad_ref, hid_ref, gain_ref, back_ref, out_ref, gate_ref):
    tokens, width = grad_ref.shape
    rows = back_ref.shape[0]
    experts = rows // SLOTS
    quarter = width // PARTS
    ids = ids_ref[...]
    weights = weight_ref[...]
    top = ids.shape[1]
    lane = iota((tokens, experts), 1)
    weight = jnp.zeros((tokens, experts), F32)
    for k in range(top):
        weight = weight + jnp.where(ids[:, k : k + 1] == lane, weights[:, k : k + 1], 0.0)
    slot = per_row(routing(ids, experts).T)
    weight = per_row(weight.T)
    place = iota(slot.shape, 0) & (SLOTS - 1)
    first = slot == place.astype(F32)
    late = slot == (SLOTS + (place >> 2)).astype(F32)
    high = weight.astype(BF).astype(F32)
    low = weight - high
    pick = jnp.concatenate(
        [jnp.where(first, high, 0.0).astype(BF), jnp.where(first, low, 0.0).astype(BF)], axis=1
    )
    moe = dot_tn(pick, back_ref[:, :width])
    moe = moe[:tokens] + moe[tokens:]
    pick_late = jnp.concatenate(
        [
            jnp.where(late & ((place & (PARTS - 1)) == part), value, 0.0).astype(BF)
            for part in range(PARTS)
            for value in (high, low)
        ],
        axis=1,
    )
    moe_late = dot_tn(pick_late, back_ref[:, width : width + quarter])
    moe_late = jnp.concatenate(
        [
            moe_late[2 * part * tokens : (2 * part + 1) * tokens]
            + moe_late[(2 * part + 1) * tokens : (2 * part + 2) * tokens]
            for part in range(PARTS)
        ],
        axis=1,
    )
    moe = moe + moe_late
    hid = hid_ref[...].astype(F32)
    inv_rms = lax.rsqrt(jnp.mean(hid * hid, axis=1, keepdims=True) + 1e-06)
    normal = hid * inv_rms
    scaled = moe * gain_ref[...]
    inner_mean = jnp.mean(scaled * normal, axis=1, keepdims=True)
    out_ref[...] = (grad_ref[...].astype(F32) + inv_rms * (scaled - normal * inner_mean)).astype(BF)
    score = back_ref[:, width + quarter :].astype(F32)
    got = jnp.where(first, score[:, 0:1], 0.0) + jnp.where(
        late & ((place & (PARTS - 1)) == 0), score[:, 1:2], 0.0
    )
    by_expert = jnp.sum(got.reshape(experts, SLOTS, tokens), axis=1).T
    column = iota((tokens, top), 1)
    gate = jnp.zeros((tokens, top), F32)
    for k in range(top):
        value = jnp.sum(jnp.where(ids[:, k : k + 1] == lane, by_expert, 0.0), axis=1, keepdims=True)
        gate = gate + jnp.where(column == k, value, 0.0)
    gate_ref[...] = gate.astype(BF)


def combine(ids, weights, grad_out, hidden_in, gain, back):
    return pl.pallas_call(
        combine_kernel,
        out_shape=(
            jax.ShapeDtypeStruct(grad_out.shape, BF),
            jax.ShapeDtypeStruct(ids.shape, BF),
        ),
        compiler_params=pltpu.CompilerParams(vmem_limit_bytes=48 << 20),
        name="combine",
    )(ids, weights, grad_out, hidden_in, gain, back)


def attention_kernel(hidden_ref, proj_ref, q_ref, k_ref, v_ref, dq_ref, dk_ref, dv_ref, acc_k, acc_v):
    length = q_ref.shape[0]
    scale = HD ** (-0.5)
    block = 256
    grad_all = dot_nt(hidden_ref[...], proj_ref[...]).astype(BF)
    for i in range(length // block):
        lo, hi = i * block, (i + 1) * block
        query = q_ref[lo:hi, :]
        grad = grad_all[lo:hi]
        keys = k_ref[:hi, :]
        scores = dot_nt(keys, query)
        corner = jnp.where(
            iota((block, block), 0) <= iota((block, block), 1), scores[lo:hi], -jnp.inf
        )
        scores = jnp.concatenate([scores[:lo], corner], axis=0) if i else corner
        peak = jnp.max(scores, axis=0, keepdims=True)
        exp_scores = jnp.exp((scores - peak) * scale)
        probs = exp_scores * (1.0 / jnp.sum(exp_scores, axis=0, keepdims=True))
        grad_probs = dot_nt(v_ref[:hi, :], grad)
        delta = jnp.sum(probs * grad_probs, axis=0, keepdims=True)
        grad_scores = (probs * (grad_probs - delta)).astype(BF)
        dq_ref[lo:hi, :] = (scale * dot_tn(grad_scores, keys)).astype(BF)
        dv = dot_nn(probs.astype(BF), grad)
        dk = dot_nn(grad_scores, query)
        if i:
            acc_k[:lo, :] += dk[:lo]
            acc_v[:lo, :] += dv[:lo]
        acc_k[lo:hi, :] = dk[lo:]
        acc_v[lo:hi, :] = dv[lo:]
    dk_ref[...] = (scale * acc_k[...]).astype(BF)
    dv_ref[...] = acc_v[...].astype(BF)


def attention(hidden, proj, query, key, value):
    tokens, cols = query.shape
    length = tokens // SEQS
    width = hidden.shape[1]
    item = pl.BlockSpec((length, HD), lambda s, h: (s, h))
    return pl.pallas_call(
        attention_kernel,
        out_shape=[jax.ShapeDtypeStruct(query.shape, BF)] * 3,
        grid=(SEQS, cols // HD),
        in_specs=[
            pl.BlockSpec((length, width), lambda s, h: (s, 0)),
            pl.BlockSpec((HD, width), lambda s, h: (h, 0)),
            item,
            item,
            item,
        ],
        out_specs=[item] * 3,
        scratch_shapes=[pltpu.VMEM((length, HD), F32), pltpu.VMEM((length, HD), F32)],
        compiler_params=pltpu.CompilerParams(vmem_limit_bytes=48 << 20),
        name="attention",
    )(hidden, proj, query, key, value)


def exchange(rows, experts):
    total = rows.shape[1]
    moved = lax.all_to_all(
        rows.reshape(experts, SLOTS, total),
        ("group", "inner"),
        split_axis=0,
        concat_axis=0,
        tiled=True,
    )
    return moved.reshape(experts * SLOTS, total)


def local(
    grad_out,
    hidden_in,
    norm_gain,
    expert_ids,
    gate_weights,
    gate_proj,
    up_proj,
    down_proj,
    out_proj,
    query_rows,
    key_rows,
    value_rows,
):
    experts = lax.axis_size("group") * lax.axis_size("inner")
    gain = norm_gain.reshape(1, -1)
    outgoing = dispatch(expert_ids, grad_out, hidden_in, gain, experts)
    arrived = exchange(outgoing, experts)
    answers = expert_backward(arrived, gate_proj[0], up_proj[0], down_proj[0])
    back = exchange(answers, experts)
    grad_hidden, grad_gate = combine(
        expert_ids, gate_weights, grad_out, hidden_in, gain, back
    )
    gathered = lax.all_gather(grad_hidden, "inner", axis=0, tiled=True)
    grad_q, grad_k, grad_v = attention(gathered, out_proj, query_rows, key_rows, value_rows)
    return (grad_hidden, grad_gate, grad_q, grad_k, grad_v)


def solution(mesh):
    rows = P(("group", "inner"), None)
    stack = P(("group", "inner"), None, None)
    heads = P("group", "inner")
    return jax.shard_map(
        local,
        mesh=mesh,
        in_specs=(
            rows,
            rows,
            P(),
            rows,
            rows,
            stack,
            stack,
            stack,
            P("inner", None),
            heads,
            heads,
            heads,
        ),
        out_specs=(rows, rows, heads, heads, heads),
        check_vma=False,
    )
```

time: 615 us -> 364 us (0.59); the launches traced: 607 us -> 362 us
  local copies, waits for them, and re-layouts: 115 us -> 6.8 us
  matrix products: 93.2 us -> 0 us
  Pallas kernels: 0 us -> 72 us
  blocking collectives: 200 us -> 131 us
  other arithmetic: 16.2 us -> 0 us
  waiting for transfers between devices: 149 us -> 133 us
  starting transfers between devices: 17.6 us -> 6.17 us
    dot_general x27 -> x0, matrix products: 93.2 us -> none  [the longest x12 51 us: dot_rt(): lax.dot_general(left, right, (((1,), (1,)), ((), ())), preferred_element_...]
    pallas_call x0 -> x4, Pallas kernels: none -> 72 us  [the longest x1 32.9 us: expert_backward(): pl.pallas_call(expert_kernel, out_shape=jax.ShapeDtypeStruct((rows, out_w...]
    all_to_all x1, blocking collectives: 200 us -> 131 us  [exchange(): lax.all_to_all(rows.reshape(experts, SLOTS, total), ('group', 'inner'), s...]
    reshape x17 -> x0, local copies, waits for them, and re-layouts: 64.8 us -> none  [the longest x1 16.5 us: local(): arrived = arrived.reshape(experts * capacity, 2 * model_width)]
    all_to_all x2 -> x1, waiting for transfers between devices: 105 us -> 65.5 us  [exchange(): lax.all_to_all(rows.reshape(experts, SLOTS, total), ('group', 'inner'), s...]
    gather x3 -> x0, local copies, waits for them, and re-layouts: 38.9 us -> none  [the longest x1 20.2 us: local(): outgoing = send_rows[owner_token]]
    all_gather x1, waiting for transfers between devices: 44 us -> 67.1 us  [local(): gathered = lax.all_gather(grad_hidden, 'inner', axis=0, tiled=True)]
    all_to_all x2 -> x1, starting transfers between devices: 17.6 us -> 5.95 us  [exchange(): lax.all_to_all(rows.reshape(experts, SLOTS, total), ('group', 'inner'), s...]
  transfers between devices with their start and end apart: 3 -> 2, of which waited for: 3 -> 2; matrix products, arithmetic and copies ran while one was open for 2% -> 0% of each run, Pallas kernels for 0% -> 0%
where the time goes in v1:
time: 364 us; the launch traced here: 362 us
  waiting for transfers between devices  133 us (37%)
  blocking collectives  131 us (36%)
  Pallas kernels  72 us (20%)
  between operations  14.1 us (4%)
  local copies, waits for them, and re-layouts  6.8 us (2%)
  starting transfers between devices  6.17 us (2%)
    all_to_all x1, blocking collectives, exchange(): lax.all_to_all(rows.reshape(experts, SLOTS, total), ('group', 'inner'), s...  131 us
    all_gather x1, waiting for transfers between devices, local(): gathered = lax.all_gather(grad_hidden, 'inner', axis=0, tiled=True)  67.1 us
    all_to_all x1, waiting for transfers between devices, exchange(): lax.all_to_all(rows.reshape(experts, SLOTS, total), ('group', 'inner'), s...  65.5 us
    pallas_call x1, Pallas kernels, expert_backward(): pl.pallas_call(expert_kernel, out_shape=jax.ShapeDtypeStruct((rows, out_w...  32.9 us
    pallas_call x1, Pallas kernels, attention(): pl.pallas_call(attention_kernel, out_shape=[jax.ShapeDtypeStruct(query.sh...  27.3 us
  transfers between devices with their start and end apart: 2, of which 2 were waited for; matrix products, arithmetic and copies ran while one was open for 0% of the time, Pallas kernels for 0%

profile of v1, /device:TPU:0, one launch (start us, length us, event | category | flops | bytes accessed | tf_op | source)
XLA Modules:
  0.0 362.3 jit_solution(504296016303761248)
XLA Ops:
  7.2 0.8 copy.18.ids_ref
  8.0 0.0 copy-start
  8.0 1.0 copy-done
  9.0 0.0 copy-start.2
  9.0 1.0 copy-done.2
  10.0 0.0 copy-start.8
  10.0 0.7 copy-done.8
  10.7 4.6 %dispatch.1 = bf16[1024,5120]{1,0:T(8,128)(2,1)S(1)} custom-call(s32[128,8]{1,0:T(8,128)S(1)} %copy.18.ids_ref, bf16[128,2048]{1,0:T(8,128)(2,1)S(1)} %copy-done, bf16[128,2048]{1,0:T(8,128)(2,1)S(1)} %copy-done.2, f32[1,2048]{1,0:T(1,128)S(1)} %bitcast.9), custom_call_target="tpu_custom_call" | custom-call | tf_op jit(solution)/shard_map/dispatch/pallas_call | solution.py:103
  15.4 130.6 %all_to_all.10 = bf16[128,8,5120]{2,1,0:T(8,128)(2,1)} all-to-all(bf16[128,8,5120]{2,1,0:T(8,128)(2,1)S(1)} %bitcast.8), channel_id=1, replica_groups=mesh['group'=8,'inner'=16] {'group','inner'}, dimensions={0} | all-to-all | bytes 20971520 | tf_op jit(solution)/shard_map/all_to_all | solution.py:327
  146.0 32.9 %expert.1 = bf16[1024,2688]{1,0:T(8,128)(2,1)} custom-call(bf16[1024,5120]{1,0:T(8,128)(2,1)} %bitcast.11, bf16[2048,768]{1,0:T(8,128)(2,1)} %bitcast.13, bf16[2048,768]{1,0:T(8,128)(2,1)} %bitcast.14, bf16[768,2048]{1,0:T(8,128)(2,1)} %bitcast.15), custom_call_target="tpu_custom_call" | custom-call | tf_op jit(solution)/shard_map/expert/pallas_call | solution.py:179
  178.9 0.0 copy-start.10
  178.9 0.0 copy-start.1
  178.9 0.0 copy-start.9
  178.9 5.9 %all-to-all-start.1 = ((bf16[128,8,2688]{2,1,0:T(8,128)(2,1)}), bf16[128,8,2688]{2,1,0:T(8,128)(2,1)}, u32[]{:S(2)}, u32[]{:S(2)}) async-start(bf16[128,8,2688]{2,1,0:T(8,128)(2,1)} %bitcast.12), calls=%async_computation.1 | async-start | bytes 11010048 | tf_op jit(solution)/shard_map/all_to_all | solution.py:327
  184.9 0.0 copy-start.4
  184.9 0.0 copy-start.5
  184.9 0.2 all-gather.2.cloned.1.call-start
  185.2 0.0 copy-done.10
  185.2 0.1 copy.19.weight_ref
  185.3 65.5 %all-to-all-done.1 = bf16[128,8,2688]{2,1,0:T(8,128)(2,1)} async-done(((bf16[128,8,2688]{2,1,0:T(8,128)(2,1)}), bf16[128,8,2688]{2,1,0:T(8,128)(2,1)}, u32[]{:S(2)}, u32[]{:S(2)}) %all-to-all-start.1) | async-done | bytes 5505056 | tf_op jit(solution)/shard_map/all_to_all | solution.py:327
  250.8 0.0 copy-done.1
  250.8 0.0 copy-done.3
  250.8 0.0 copy-done.9
  250.8 7.2 %combine.1 = (bf16[128,2048]{1,0:T(8,128)(2,1)}, bf16[128,8]{1,0:T(8,128)(2,1)S(1)}) custom-call(s32[128,8]{1,0:T(8,128)S(1)} %copy.18.ids_ref, f32[128,8]{1,0:T(8,128)S(1)} %copy.19.weight_ref, bf16[128,2048]{1,0:T(8,128)(2,1)S(1)} %copy-done.1, bf16[128,2048]{1,0:T(8,128)(2,1)S(1)} %copy-done.3, f32[1,2048]{1,0:T(1,128)S(1)} %bitcast.10, ...), custom_call_target="tpu_custom_call" | custom-call | tf_op jit(solution)/shard_map/combine/pallas_call | solution.py:258
  257.9 0.0 all-gather.2.cloned.1.call-update
  258.0 0.7 copy.20
  258.6 67.1 %all-gather.2.cloned.1.call-done.hidden_ref = bf16[2048,2048]{1,0:T(8,128)(2,1)} async-done(((bf16[128,2048]{1,0:T(8,128)(2,1)}), bf16[2048,2048]{1,0:T(8,128)(2,1)}) %all-gather.2.cloned.1.call-update) | async-done | bytes 8388624 | tf_op jit(solution)/shard_map/all_gather | solution.py:360
  325.8 0.0 copy-done.4
  325.8 0.0 copy-done.5
  325.8 1.2 copy-done.6
  327.0 1.2 copy-done.7
  328.2 27.3 %attention.1 = (bf16[2048,256]{1,0:T(8,128)(2,1)}, bf16[2048,256]{1,0:T(8,128)(2,1)}, bf16[2048,256]{1,0:T(8,128)(2,1)}) custom-call(bf16[2048,2048]{1,0:T(8,128)(2,1)} %all-gather.2.cloned.1.call-done.hidden_ref, bf16[256,2048]{1,0:T(8,128)(2,1)S(1)} %copy-done.4, bf16[2048,256]{1,0:T(8,128)(2,1)S(1)} %copy-done.5, bf16[2048,256]{1,0:T(8,128)(2,1)S(1)} %copy-done.6, ...), custom_call_target="tpu_custom_call" | custom-call | tf_op jit(solution)/shard_map/attention/pallas_call | solution.py:307
  (3 shorter events, 0.0 us)
Async XLA Ops:
  8.0 1.0 copy-start
  9.0 1.0 copy-start.2
  10.0 0.7 copy-start.8
  178.9 6.2 %copy-start.10 = (f32[128,8]{0,1:T(8,128)S(1)}, f32[128,8]{0,1:T(8,128)}, u32[]{:S(2)}) copy-start(f32[128,8]{0,1:T(8,128)} %param.16) | copy-start | bytes 12292
  178.9 71.8 %copy-start.1 = (bf16[128,2048]{1,0:T(8,128)(2,1)S(1)}, bf16[128,2048]{1,0:T(8,128)(2,1)}, u32[]{:S(2)}) copy-start(bf16[128,2048]{1,0:T(8,128)(2,1)} %grad_ref.3) | copy-start | bytes 1572868
  178.9 71.8 %copy-start.3 = (bf16[128,2048]{1,0:T(8,128)(2,1)S(1)}, bf16[128,2048]{1,0:T(8,128)(2,1)}, u32[]{:S(2)}) copy-start(bf16[128,2048]{1,0:T(8,128)(2,1)} %hid_ref.3) | copy-start | bytes 1572868
  178.9 71.8 %copy-start.9 = (f32[2048]{0:T(1024)S(1)}, f32[2048]{0:T(1024)}, u32[]{:S(2)}) copy-start(f32[2048]{0:T(1024)} %param.14) | copy-start | bytes 24580
  178.9 71.8 %all-to-all-start.1 = ((bf16[128,8,2688]{2,1,0:T(8,128)(2,1)}), bf16[128,8,2688]{2,1,0:T(8,128)(2,1)}, u32[]{:S(2)}, u32[]{:S(2)}) async-start(bf16[128,8,2688]{2,1,0:T(8,128)(2,1)} %bitcast.12), calls=%async_computation.1 | async-start | bytes 11010048 | tf_op jit(solution)/shard_map/all_to_all | solution.py:327
  184.9 140.8 %copy-start.4 = (bf16[256,2048]{1,0:T(8,128)(2,1)S(1)}, bf16[256,2048]{1,0:T(8,128)(2,1)}, u32[]{:S(2)}) copy-start(bf16[256,2048]{1,0:T(8,128)(2,1)} %proj_ref.1) | copy-start | bytes 3145732
  184.9 140.8 %copy-start.5 = (bf16[2048,256]{1,0:T(8,128)(2,1)S(1)}, bf16[2048,256]{1,0:T(8,128)(2,1)}, u32[]{:S(2)}) copy-start(bf16[2048,256]{1,0:T(8,128)(2,1)} %q_ref.1) | copy-start | bytes 3145732
  184.9 140.8 %all-gather.2.cloned.1.call-start = ((), (), s32[]{:S(2)}) async-start(), calls=%async_computation.2 | async-start | bytes 8912896 | tf_op jit(solution)/shard_map/all_gather | solution.py:360
  325.8 1.2 copy-start.6
  327.0 1.2 copy-start.7
Sparse Core Ops, SparseCore 0:
  258.1 67.6 all-gather.1

commit v2 on v1

--- a/solution.py
+++ b/solution.py
@@ -121,11 +121,26 @@
     )(ids, grad_out, hidden_in, gain)
 
 
-def expert_kernel(rows_ref, gate_ref, up_ref, down_ref, out_ref, grad_ref, norm_ref):
+def expert_kernel(
+    rows_ref, gate_hbm, up_hbm, down_hbm, out_ref, grad_ref, norm_ref, gate_ref, up_ref, down_ref, sems
+):
     width = gate_ref.shape[0]
     main = rows_ref.shape[0]
     late = main // SLOTS * EXTRA
     half = width // 2
+    step = pl.program_id(0)
+    loads = [
+        pltpu.make_async_copy(gate_hbm, gate_ref, sems.at[0]),
+        pltpu.make_async_copy(up_hbm, up_ref, sems.at[1]),
+        pltpu.make_async_copy(down_hbm, down_ref, sems.at[2]),
+    ]
+
+    def first(action):
+        @pl.when(step == 0)
+        def _():
+            action()
+
+    first(lambda: [load.start() for load in loads])
     grad_ref[:main, :] = rows_ref[:, :width]
     norm_ref[:main, :] = rows_ref[:, width : 2 * width]
     order = iota((main, main), 0)
@@ -136,12 +151,14 @@
         cols = slice(part * half, (part + 1) * half)
         grad_ref[main:, cols] = moved[part * late : (part + 1) * late]
         norm_ref[main:, cols] = moved[(2 + part) * late : (3 + part) * late]
-    norm = norm_ref[...]
-    gate_pre = dot_nn(norm, gate_ref[...])
-    up_pre = dot_nn(norm, up_ref[...])
+    first(loads[0].wait)
+    gate_pre = dot_nn(norm_ref[...], gate_ref[...])
+    first(loads[1].wait)
+    up_pre = dot_nn(norm_ref[...], up_ref[...])
     sigma = jax.nn.sigmoid(gate_pre)
     act = gate_pre * sigma
     slope = sigma * (1.0 + gate_pre * (1.0 - sigma))
+    first(loads[2].wait)
     grad_hid = dot_nt(grad_ref[...], down_ref[...])
     grad_uppre = grad_hid * act
     score = jnp.sum(grad_uppre * up_pre, axis=1, keepdims=True)
@@ -166,34 +183,33 @@
     ).astype(BF)
 
 
-def expert_backward(arrived, gate_mat, up_mat, down_mat):
+def expert_backward(arrived, gate_mat, up_mat, down_mat, steps=4):
     rows, total = arrived.shape
-    width, hidden = gate_mat.shape
-    steps = 2
+    width = gate_mat.shape[0]
     main = rows // steps
     both = main + main // SLOTS * EXTRA
     out_width = width + width // PARTS + LANES
-    fixed = lambda shape: pl.BlockSpec(
-        shape, lambda i: (0,) * len(shape), pipeline_mode=pl.Buffered(1)
-    )
+    raw = pl.BlockSpec(memory_space=pl.ANY)
     return pl.pallas_call(
         expert_kernel,
         out_shape=jax.ShapeDtypeStruct((rows, out_width), BF),
         grid=(steps,),
-        in_specs=[
-            pl.BlockSpec((main, total), lambda i: (i, 0)),
-            fixed(gate_mat.shape),
-            fixed(up_mat.shape),
-            fixed(down_mat.shape),
-        ],
+        in_specs=[pl.BlockSpec((main, total), lambda i: (i, 0)), raw, raw, raw],
         out_specs=pl.BlockSpec((main, out_width), lambda i: (i, 0)),
-        scratch_shapes=[pltpu.VMEM((both, width), BF), pltpu.VMEM((both, width), BF)],
+        scratch_shapes=[
+            pltpu.VMEM((both, width), BF),
+            pltpu.VMEM((both, width), BF),
+            pltpu.VMEM(gate_mat.shape, BF),
+            pltpu.VMEM(up_mat.shape, BF),
+            pltpu.VMEM(down_mat.shape, BF),
+            pltpu.SemaphoreType.DMA((3,)),
+        ],
         compiler_params=pltpu.CompilerParams(vmem_limit_bytes=56 << 20),
         name="expert",
     )(arrived, gate_mat, up_mat, down_mat)
 
 
-def combine_kernel(ids_ref, weight_ref, grad_ref, hid_ref, gain_ref, back_ref, out_ref, gate_ref):
+def combine_rows(ids_ref, weight_ref, grad_ref, hid_ref, gain_ref, back_ref, out_ref, gate_ref):
     tokens, width = grad_ref.shape
     rows = back_ref.shape[0]
     experts = rows // SLOTS
@@ -254,43 +270,127 @@
     gate_ref[...] = gate.astype(BF)
 
 
-def combine(ids, weights, grad_out, hidden_in, gain, back):
+def combine_kernel(
+    ids_ref,
+    weight_ref,
+    grad_ref,
+    hid_ref,
+    gain_ref,
+    back_ref,
+    proj_ref,
+    out_ref,
+    gate_ref,
+    attn_ref,
+):
+    @pl.when(pl.program_id(0) == 0)
+    def _():
+        combine_rows(
+            ids_ref, weight_ref, grad_ref, hid_ref, gain_ref, back_ref, out_ref, gate_ref
+        )
+
+    pieces, _, piece, width = proj_ref.shape
+    owners, heads, tokens, _ = attn_ref.shape
+    each = pieces // owners
+    for owner in range(owners):
+        proj = proj_ref[:, owner].reshape(pieces * piece, width)
+        grad = dot_nt(out_ref[...], proj).astype(BF)
+        for head in range(heads):
+            attn_ref[owner, head] = grad[:, head * HD : (head + 1) * HD]
+
+
+def combine(ids, weights, grad_out, hidden_in, gain, back, proj):
+    tokens, width = grad_out.shape
+    pieces, owners, piece, _ = proj.shape
+    heads = pieces * piece // HD
+    group = 2
+    whole = lambda shape: pl.BlockSpec(shape, lambda i: (0,) * len(shape))
     return pl.pallas_call(
         combine_kernel,
         out_shape=(
             jax.ShapeDtypeStruct(grad_out.shape, BF),
             jax.ShapeDtypeStruct(ids.shape, BF),
+            jax.ShapeDtypeStruct((owners, heads, tokens, HD), BF),
+        ),
+        grid=(owners // group,),
+        in_specs=[
+            whole(ids.shape),
+            whole(weights.shape),
+            whole(grad_out.shape),
+            whole(hidden_in.shape),
+            whole(gain.shape),
+            whole(back.shape),
+            pl.BlockSpec((pieces, group, piece, width), lambda i: (0, i, 0, 0)),
+        ],
+        out_specs=(
+            whole(grad_out.shape),
+            whole(ids.shape),
+            pl.BlockSpec((group, heads, tokens, HD), lambda i: (i, 0, 0, 0)),
         ),
         compiler_params=pltpu.CompilerParams(vmem_limit_bytes=48 << 20),
         name="combine",
-    )(ids, weights, grad_out, hidden_in, gain, back)
-
-
-def attention_kernel(hidden_ref, proj_ref, q_ref, k_ref, v_ref, dq_ref, dk_ref, dv_ref, acc_k, acc_v):
+    )(ids, weights, grad_out, hidden_in, gain, back, proj)
+
+
+BLOCK = 256
+
+
+def probs_kernel(q_ref, k_ref, out_ref):
     length = q_ref.shape[0]
     scale = HD ** (-0.5)
-    block = 256
-    grad_all = dot_nt(hidden_ref[...], proj_ref[...]).astype(BF)
-    for i in range(length // block):
-        lo, hi = i * block, (i + 1) * block
+    start = 0
+    for lo in range(0, length, BLOCK):
+        hi = lo + BLOCK
+        scores = dot_nt(k_ref[:hi, :], q_ref[lo:hi, :])
+        corner = jnp.where(
+            iota((BLOCK, BLOCK), 0) <= iota((BLOCK, BLOCK), 1), scores[lo:], -jnp.inf
+        )
+        scores = jnp.concatenate([scores[:lo], corner], axis=0) if lo else corner
+        peak = jnp.max(scores, axis=0, keepdims=True)
+        exp_scores = jnp.exp((scores - peak) * scale)
+        total = jnp.sum(exp_scores, axis=0, keepdims=True)
+        out_ref[start : start + hi, :] = (exp_scores * (1.0 / total)).astype(BF)
+        start += hi
+
+
+def packed_rows(length):
+    return sum(range(BLOCK, length + 1, BLOCK))
+
+
+def attention_probs(query, key):
+    tokens, cols = query.shape
+    length = tokens // SEQS
+    heads = cols // HD
+    item = pl.BlockSpec((length, HD), lambda s, h: (s, h))
+    return pl.pallas_call(
+        probs_kernel,
+        out_shape=jax.ShapeDtypeStruct((SEQS, heads, packed_rows(length), BLOCK), BF),
+        grid=(SEQS, heads),
+        in_specs=[item, item],
+        out_specs=pl.BlockSpec((None, None, packed_rows(length), BLOCK), lambda s, h: (s, h, 0, 0)),
+        compiler_params=pltpu.CompilerParams(vmem_limit_bytes=32 << 20),
+        name="probs",
+    )(query, key)
+
+
+def attention_kernel(probs_ref, grad_ref, q_ref, k_ref, v_ref, dq_ref, dk_ref, dv_ref, acc_k, acc_v):
+    length = q_ref.shape[0]
+    scale = HD ** (-0.5)
+    grad_all = grad_ref[...].reshape(length, HD)
+    start = 0
+    for lo in range(0, length, BLOCK):
+        hi = lo + BLOCK
         query = q_ref[lo:hi, :]
         grad = grad_all[lo:hi]
-        keys = k_ref[:hi, :]
-        scores = dot_nt(keys, query)
-        corner = jnp.where(
-            iota((block, block), 0) <= iota((block, block), 1), scores[lo:hi], -jnp.inf
-        )
-        scores = jnp.concatenate([scores[:lo], corner], axis=0) if i else corner
-        peak = jnp.max(scores, axis=0, keepdims=True)
-        exp_scores = jnp.exp((scores - peak) * scale)
-        probs = exp_scores * (1.0 / jnp.sum(exp_scores, axis=0, keepdims=True))
+        probs = probs_ref[start : start + hi, :]
+        start += hi
+        full = probs.astype(F32)
         grad_probs = dot_nt(v_ref[:hi, :], grad)
-        delta = jnp.sum(probs * grad_probs, axis=0, keepdims=True)
-        grad_scores = (probs * (grad_probs - delta)).astype(BF)
-        dq_ref[lo:hi, :] = (scale * dot_tn(grad_scores, keys)).astype(BF)
-        dv = dot_nn(probs.astype(BF), grad)
+        delta = jnp.sum(full * grad_probs, axis=0, keepdims=True)
+        grad_scores = (full * (grad_probs - delta)).astype(BF)
+        dq_ref[lo:hi, :] = (scale * dot_tn(grad_scores, k_ref[:hi, :])).astype(BF)
+        dv = dot_nn(probs, grad)
         dk = dot_nn(grad_scores, query)
-        if i:
+        if lo:
             acc_k[:lo, :] += dk[:lo]
             acc_v[:lo, :] += dv[:lo]
         acc_k[lo:hi, :] = dk[lo:]
@@ -299,27 +399,27 @@
     dv_ref[...] = acc_v[...].astype(BF)
 
 
-def attention(hidden, proj, query, key, value):
+def attention(probs, grad_attn, query, key, value):
     tokens, cols = query.shape
     length = tokens // SEQS
-    width = hidden.shape[1]
+    owners, _, part, _ = grad_attn.shape
     item = pl.BlockSpec((length, HD), lambda s, h: (s, h))
     return pl.pallas_call(
         attention_kernel,
         out_shape=[jax.ShapeDtypeStruct(query.shape, BF)] * 3,
         grid=(SEQS, cols // HD),
         in_specs=[
-            pl.BlockSpec((length, width), lambda s, h: (s, 0)),
-            pl.BlockSpec((HD, width), lambda s, h: (h, 0)),
+            pl.BlockSpec((None, None) + probs.shape[2:], lambda s, h: (s, h, 0, 0)),
+            pl.BlockSpec((owners // SEQS, None, part, HD), lambda s, h: (s, h, 0, 0)),
             item,
             item,
             item,
         ],
         out_specs=[item] * 3,
         scratch_shapes=[pltpu.VMEM((length, HD), F32), pltpu.VMEM((length, HD), F32)],
-        compiler_params=pltpu.CompilerParams(vmem_limit_bytes=48 << 20),
+        compiler_params=pltpu.CompilerParams(vmem_limit_bytes=32 << 20),
         name="attention",
-    )(hidden, proj, query, key, value)
+    )(probs, grad_attn, query, key, value)
 
 
 def exchange(rows, experts):
@@ -348,17 +448,41 @@
     key_rows,
     value_rows,
 ):
-    experts = lax.axis_size("group") * lax.axis_size("inner")
+    groups = lax.axis_size("group")
+    owners = lax.axis_size("inner")
+    experts = groups * owners
     gain = norm_gain.reshape(1, -1)
+    tokens, width = grad_out.shape
+    piece = out_proj.shape[0] // groups
+    own_proj = lax.dynamic_slice_in_dim(out_proj, lax.axis_index("group") * piece, piece, 0)
+    proj = lax.all_gather(own_proj, ("group", "inner"), axis=0, tiled=False)
     outgoing = dispatch(expert_ids, grad_out, hidden_in, gain, experts)
+    outgoing, query_late = lax.optimization_barrier((outgoing, query_rows))
     arrived = exchange(outgoing, experts)
+    probs = attention_probs(query_late, key_rows)
+    arrived, probs = lax.optimization_barrier((arrived, probs))
     answers = expert_backward(arrived, gate_proj[0], up_proj[0], down_proj[0])
     back = exchange(answers, experts)
-    grad_hidden, grad_gate = combine(
-        expert_ids, gate_weights, grad_out, hidden_in, gain, back
-    )
-    gathered = lax.all_gather(grad_hidden, "inner", axis=0, tiled=True)
-    grad_q, grad_k, grad_v = attention(gathered, out_proj, query_rows, key_rows, value_rows)
+    grad_hidden, grad_gate, grad_attn = combine(
+        expert_ids,
+        gate_weights,
+        grad_out,
+        hidden_in,
+        gain,
+        back,
+        proj.reshape(groups, owners, piece, width),
+    )
+    heads = grad_attn.shape[1]
+    grad_attn = lax.all_to_all(
+        grad_attn.reshape(owners, heads * tokens, HD),
+        "inner",
+        split_axis=0,
+        concat_axis=0,
+        tiled=True,
+    )
+    grad_q, grad_k, grad_v = attention(
+        probs, grad_attn.reshape(owners, heads, tokens, HD), query_rows, key_rows, value_rows
+    )
     return (grad_hidden, grad_gate, grad_q, grad_k, grad_v)
 
 

time: 364 us -> 347 us (0.953)
  blocking collectives: 131 us -> 0 us
  waiting for transfers between devices: 133 us -> 208 us
  starting transfers between devices: 6.17 us -> 29.4 us
  local copies, waits for them, and re-layouts: 6.8 us -> 19.2 us
  Pallas kernels: 72 us -> 75.7 us
    all_to_all x1 -> x0, blocking collectives: 131 us -> none  [exchange(): lax.all_to_all(rows.reshape(experts, SLOTS, total), ('group', 'inner'), s...]
    all_to_all x1 -> x2, waiting for transfers between devices: 65.5 us -> 190 us  [exchange(): lax.all_to_all(rows.reshape(experts, SLOTS, total), ('group', 'inner'), s...]
    all_gather x1, waiting for transfers between devices: 67.1 us -> 0.01 us  [local(): proj = lax.all_gather(own_proj, ('group', 'inner'), axis=0, tiled=False)]
    all_to_all x1 -> x2, starting transfers between devices: 5.95 us -> 24.9 us  [exchange(): lax.all_to_all(rows.reshape(experts, SLOTS, total), ('group', 'inner'), s...]
    all_to_all x0 -> x1, waiting for transfers between devices: none -> 17.7 us  [local(): lax.all_to_all(grad_attn.reshape(owners, heads * tokens, HD), 'inner', sp...]
    pallas_call x1, Pallas kernels: 27.3 us -> 11.7 us  [attention(): pl.pallas_call(attention_kernel, out_shape=[jax.ShapeDtypeStruct(query.sh...]
    unnamed x25 -> x35, local copies, waits for them, and re-layouts: 6.8 us -> 18.5 us
    pallas_call x1, Pallas kernels: 7.17 us -> 17.1 us  [combine(): pl.pallas_call(combine_kernel, out_shape=(jax.ShapeDtypeStruct(grad_out.s...]
  transfers between devices with their start and end apart: 2 -> 4, of which waited for: 2 -> 3; matrix products, arithmetic and copies ran while one was open for 0% -> 0% of each run, Pallas kernels for 0% -> 14%
where the time goes in v2:
time: 347 us
  waiting for transfers between devices  208 us (60%)
  Pallas kernels  75.7 us (22%)
  starting transfers between devices  29.4 us (8%)
  local copies, waits for them, and re-layouts  19.2 us (6%)
  between operations  14.2 us (4%)
    all_to_all x2, waiting for transfers between devices, exchange(): lax.all_to_all(rows.reshape(experts, SLOTS, total), ('group', 'inner'), s...  190 us
    pallas_call x1, Pallas kernels, expert_backward(): pl.pallas_call(expert_kernel, out_shape=jax.ShapeDtypeStruct((rows, out_w...  37.5 us
    all_to_all x2, starting transfers between devices, exchange(): lax.all_to_all(rows.reshape(experts, SLOTS, total), ('group', 'inner'), s...  24.9 us
    unnamed x35, local copies, waits for them, and re-layouts  18.5 us
    all_to_all x1, waiting for transfers between devices, local(): lax.all_to_all(grad_attn.reshape(owners, heads * tokens, HD), 'inner', sp...  17.7 us
    pallas_call x1, Pallas kernels, combine(): pl.pallas_call(combine_kernel, out_shape=(jax.ShapeDtypeStruct(grad_out.s...  17.1 us
    pallas_call x1, Pallas kernels, attention(): pl.pallas_call(attention_kernel, out_shape=[jax.ShapeDtypeStruct(query.sh...  11.7 us
  transfers between devices with their start and end apart: 4, of which 3 were waited for; matrix products, arithmetic and copies ran while one was open for 0% of the time, Pallas kernels for 14%

profile of v2, /device:TPU:0, one launch (start us, length us, event | category | flops | bytes accessed | tf_op | source)
XLA Modules:
  0.0 346.6 jit_solution(10808489330339573015)
XLA Ops:
  7.2 0.0 copy-start
  7.2 0.0 all-gather.3.cloned.1.call-start
  7.2 1.2 copy-done
  8.4 0.7 constant_dynamic-slice_fusion
  9.1 0.0 all-gather.3.cloned.1.call-update
  9.1 0.8 copy.18.ids_ref
  9.9 1.0 copy-done.7
  10.9 1.0 copy-done.9
  12.0 0.7 copy-done.13
  12.7 4.6 %dispatch.1 = bf16[1024,5120]{1,0:T(8,128)(2,1)S(1)} custom-call(s32[128,8]{1,0:T(8,128)S(1)} %copy.18.ids_ref, bf16[128,2048]{1,0:T(8,128)(2,1)S(1)} %copy-done.7, bf16[128,2048]{1,0:T(8,128)(2,1)S(1)} %copy-done.9, f32[1,2048]{1,0:T(1,128)S(1)} %bitcast.13), custom_call_target="tpu_custom_call" | custom-call | tf_op jit(solution)/shard_map/dispatch/pallas_call | solution.py:103
  17.3 4.0 %copy-done.2 = bf16[1024,5120]{1,0:T(8,128)(2,1)} copy-done((bf16[1024,5120]{1,0:T(8,128)(2,1)}, bf16[1024,5120]{1,0:T(8,128)(2,1)S(1)}, u32[]{:S(2)}) %copy-start.2) | copy-done | bytes 10485784
  21.3 11.6 %all-to-all-start = ((bf16[128,8,5120]{2,1,0:T(8,128)(2,1)}), bf16[128,8,5120]{2,1,0:T(8,128)(2,1)}, u32[]{:S(2)}, u32[]{:S(2)}) async-start(bf16[128,8,5120]{2,1,0:T(8,128)(2,1)} %bitcast.11), calls=%async_computation | async-start | bytes 20971520 | tf_op jit(solution)/shard_map/all_to_all | solution.py:427
  32.9 4.8 %probs.1.probs_ref = bf16[2,2,2560,256]{3,2,1,0:T(8,128)(2,1)S(1)} custom-call(bf16[2048,256]{1,0:T(8,128)(2,1)S(1)} %copy-done.5, bf16[2048,256]{1,0:T(8,128)(2,1)S(1)} %copy-done.6), custom_call_target="tpu_custom_call" | custom-call | tf_op jit(solution)/shard_map/probs/pallas_call | solution.py:364
  37.8 2.3 copy-done.3
  40.0 124.8 %all-to-all-done = bf16[128,8,5120]{2,1,0:T(8,128)(2,1)} async-done(((bf16[128,8,5120]{2,1,0:T(8,128)(2,1)}), bf16[128,8,5120]{2,1,0:T(8,128)(2,1)}, u32[]{:S(2)}, u32[]{:S(2)}) %all-to-all-start) | async-done | bytes 10485792 | tf_op jit(solution)/shard_map/all_to_all | solution.py:427
  164.8 37.5 %expert.1 = bf16[1024,2688]{1,0:T(8,128)(2,1)} custom-call(bf16[1024,5120]{1,0:T(8,128)(2,1)} %bitcast.2.rows_ref, bf16[2048,768]{1,0:T(8,128)(2,1)} %bitcast.17, bf16[2048,768]{1,0:T(8,128)(2,1)} %bitcast.18, bf16[768,2048]{1,0:T(8,128)(2,1)} %bitcast.19), custom_call_target="tpu_custom_call" | custom-call | tf_op jit(solution)/shard_map/expert/pallas_call | solution.py:193
  202.3 0.0 copy-start.15
  202.3 0.0 copy-start.14
  202.3 13.3 %all-to-all-start.1 = ((bf16[128,8,2688]{2,1,0:T(8,128)(2,1)}), bf16[128,8,2688]{2,1,0:T(8,128)(2,1)}, u32[]{:S(2)}, u32[]{:S(2)}) async-start(bf16[128,8,2688]{2,1,0:T(8,128)(2,1)} %bitcast.15), calls=%async_computation.1 | async-start | bytes 11010048 | tf_op jit(solution)/shard_map/all_to_all | solution.py:427
  215.6 0.0 copy-done.15
  215.6 0.1 copy.19.weight_ref
  215.7 65.6 %all-to-all-done.1 = bf16[128,8,2688]{2,1,0:T(8,128)(2,1)} async-done(((bf16[128,8,2688]{2,1,0:T(8,128)(2,1)}), bf16[128,8,2688]{2,1,0:T(8,128)(2,1)}, u32[]{:S(2)}, u32[]{:S(2)}) %all-to-all-start.1) | async-done | bytes 5505056 | tf_op jit(solution)/shard_map/all_to_all | solution.py:427
  281.3 1.0 copy-done.8
  282.3 1.0 copy-done.10
  283.4 17.1 %combine.1 = (bf16[128,2048]{1,0:T(8,128)(2,1)}, bf16[128,8]{1,0:T(8,128)(2,1)S(1)}, bf16[16,2,128,128]{3,2,1,0:T(8,128)(2,1)S(1)}) custom-call(s32[128,8]{1,0:T(8,128)S(1)} %copy.18.ids_ref, f32[128,8]{1,0:T(8,128)S(1)} %copy.19.weight_ref, bf16[128,2048]{1,0:T(8,128)(2,1)S(1)} %copy-done.8, bf16[128,2048]{1,0:T(8,128)(2,1)S(1)} %copy-done.10, ...), custom_call_target="tpu_custom_call" | custom-call | tf_op jit(solution)/shard_map/combine/pallas_call | solution.py:307
  300.4 1.0 copy-done.12
  301.4 4.5 %all-to-all-start.2 = ((bf16[16,256,128]{2,1,0:T(8,128)(2,1)}), bf16[16,256,128]{2,1,0:T(8,128)(2,1)}, u32[]{:S(2)}, u32[]{:S(2)}) async-start(bf16[16,256,128]{2,1,0:T(8,128)(2,1)} %bitcast.12), calls=%async_computation.2 | async-start | bytes 2097152 | tf_op jit(solution)/shard_map/all_to_all | solution.py:476
  305.9 0.7 copy.20
  306.6 17.7 %all-to-all-done.2 = bf16[16,256,128]{2,1,0:T(8,128)(2,1)} async-done(((bf16[16,256,128]{2,1,0:T(8,128)(2,1)}), bf16[16,256,128]{2,1,0:T(8,128)(2,1)}, u32[]{:S(2)}, u32[]{:S(2)}) %all-to-all-start.2) | async-done | bytes 1048608 | tf_op jit(solution)/shard_map/all_to_all | solution.py:476
  324.3 2.5 copy-done.4
  326.8 1.2 copy-done.11
  328.0 11.7 %attention.1 = (bf16[2048,256]{1,0:T(8,128)(2,1)}, bf16[2048,256]{1,0:T(8,128)(2,1)}, bf16[2048,256]{1,0:T(8,128)(2,1)}) custom-call(bf16[2,2,2560,256]{3,2,1,0:T(8,128)(2,1)S(1)} %copy-done.4, bf16[16,2,128,128]{3,2,1,0:T(8,128)(2,1)} %bitcast.10.grad_ref, bf16[2048,256]{1,0:T(8,128)(2,1)S(1)} %copy-done.5, bf16[2048,256]{1,0:T(8,128)(2,1)S(1)} %copy-done.6, ...), custom_call_target="tpu_custom_call" | custom-call | tf_op jit(solution)/shard_map/attention/pallas_call | solution.py:407
  (18 shorter events, 0.0 us)
Async XLA Ops:
  7.2 1.2 copy-start
  7.2 274.1 %all-gather.3.cloned.1.call-start = ((), (), s32[]{:S(2)}) async-start(), calls=%async_computation.3 | async-start | bytes 16908288 | tf_op jit(solution)/shard_map/all_gather | solution.py:458
  9.9 1.0 copy-start.7
  10.9 1.0 copy-start.9
  12.0 0.7 copy-start.13
  17.3 4.0 %copy-start.2 = (bf16[1024,5120]{1,0:T(8,128)(2,1)}, bf16[1024,5120]{1,0:T(8,128)(2,1)S(1)}, u32[]{:S(2)}) copy-start(bf16[1024,5120]{1,0:T(8,128)(2,1)S(1)} %dispatch.1) | copy-start | bytes 31457284
  21.3 11.6 %copy-start.5 = (bf16[2048,256]{1,0:T(8,128)(2,1)S(1)}, bf16[2048,256]{1,0:T(8,128)(2,1)}, u32[]{:S(2)}) copy-start(bf16[2048,256]{1,0:T(8,128)(2,1)} %q_ref.2) | copy-start | bytes 3145732
  21.3 11.6 %copy-start.6 = (bf16[2048,256]{1,0:T(8,128)(2,1)S(1)}, bf16[2048,256]{1,0:T(8,128)(2,1)}, u32[]{:S(2)}) copy-start(bf16[2048,256]{1,0:T(8,128)(2,1)} %k_ref.3) | copy-start | bytes 3145732
  21.3 143.6 %all-to-all-start = ((bf16[128,8,5120]{2,1,0:T(8,128)(2,1)}), bf16[128,8,5120]{2,1,0:T(8,128)(2,1)}, u32[]{:S(2)}, u32[]{:S(2)}) async-start(bf16[128,8,5120]{2,1,0:T(8,128)(2,1)} %bitcast.11), calls=%async_computation | async-start | bytes 20971520 | tf_op jit(solution)/shard_map/all_to_all | solution.py:427
  37.8 2.3 copy-start.3
  202.3 13.3 %copy-start.15 = (f32[128,8]{0,1:T(8,128)S(1)}, f32[128,8]{0,1:T(8,128)}, u32[]{:S(2)}) copy-start(f32[128,8]{0,1:T(8,128)} %param.16) | copy-start | bytes 12292
  202.3 79.0 %copy-start.14 = (f32[2048]{0:T(1024)S(1)}, f32[2048]{0:T(1024)}, u32[]{:S(2)}) copy-start(f32[2048]{0:T(1024)} %param.14) | copy-start | bytes 24580
  202.3 79.0 %all-to-all-start.1 = ((bf16[128,8,2688]{2,1,0:T(8,128)(2,1)}), bf16[128,8,2688]{2,1,0:T(8,128)(2,1)}, u32[]{:S(2)}, u32[]{:S(2)}) async-start(bf16[128,8,2688]{2,1,0:T(8,128)(2,1)} %bitcast.15), calls=%async_computation.1 | async-start | bytes 11010048 | tf_op jit(solution)/shard_map/all_to_all | solution.py:427
  281.3 1.0 copy-start.8
  282.3 1.0 copy-start.10
  300.4 1.0 copy-start.12
  301.4 38.4 %copy-start.1 = (bf16[256,2048]{1,0:T(8,128)(2,1)S(1)}, bf16[256,2048]{1,0:T(8,128)(2,1)}, u32[]{:S(2)}) copy-start(bf16[256,2048]{1,0:T(8,128)(2,1)} %param.20) | copy-start | bytes 3145732
  301.4 22.9 %all-to-all-start.2 = ((bf16[16,256,128]{2,1,0:T(8,128)(2,1)}), bf16[16,256,128]{2,1,0:T(8,128)(2,1)}, u32[]{:S(2)}, u32[]{:S(2)}) async-start(bf16[16,256,128]{2,1,0:T(8,128)(2,1)} %bitcast.12), calls=%async_computation.2 | async-start | bytes 2097152 | tf_op jit(solution)/shard_map/all_to_all | solution.py:476
  324.3 2.5 copy-start.4
  326.8 1.2 copy-start.11
Sparse Core Ops, SparseCore 0:
  11.7 184.9 all-gather.2

commit v3 on v2

v3 whole, which is shorter than its diff:
```python
import functools

import jax
import jax.numpy as jnp
from jax import lax
from jax.experimental import pallas as pl
from jax.experimental.pallas import tpu as pltpu
from jax.sharding import PartitionSpec as P

HD = 128
SEQS = 2
SLOTS = 8
EXTRA = 2
PARTS = 4
LANES = 128
BF = jnp.bfloat16
F32 = jnp.float32


def dot_nn(left, right):
    return lax.dot_general(left, right, (((1,), (0,)), ((), ())), preferred_element_type=F32)


def dot_nt(left, right):
    return lax.dot_general(left, right, (((1,), (1,)), ((), ())), preferred_element_type=F32)


def dot_tn(left, right):
    return lax.dot_general(left, right, (((0,), (0,)), ((), ())), preferred_element_type=F32)


HELD = pl.BlockSpec(memory_space=pltpu.VMEM)
RAW = pl.BlockSpec(memory_space=pl.ANY)


def kernel_call(kernel, out_shape, vmem, space=pltpu.HBM, free=(), **fields):
    outs = out_shape
    if space is not None:
        outs = jax.tree.map(lambda out: space(out.shape, out.dtype), out_shape)
    call = pl.pallas_call(
        kernel,
        out_shape=outs,
        compiler_params=pltpu.CompilerParams(vmem_limit_bytes=vmem << 20),
        **fields,
    )
    pin = lambda arg: pltpu.with_memory_space_constraint(arg, pltpu.HBM)
    return lambda *args: call(*[arg if n in free else pin(arg) for n, arg in enumerate(args)])


def iota(shape, dim):
    return lax.broadcasted_iota(jnp.int32, shape, dim)


def routing(ids, experts):
    tokens, top = ids.shape
    lane = iota((tokens, experts), 1)
    member = jnp.zeros((tokens, experts), F32)
    for k in range(top):
        member = member + jnp.where(ids[:, k : k + 1] == lane, 1.0, 0.0)
    earlier = jnp.where(iota((tokens, tokens), 1) < iota((tokens, tokens), 0), 1.0, 0.0).astype(BF)
    slot = dot_nn(earlier, member.astype(BF))
    return jnp.where(member > 0.5, slot, -1.0)


def per_row(by_expert):
    experts, width = by_expert.shape
    return jnp.broadcast_to(by_expert[:, None, :], (experts, SLOTS, width)).reshape(
        experts * SLOTS, width
    )


def dispatch_kernel(ids_ref, grad_ref, hid_ref, gain_ref, out_ref, rows_ref, parts_ref, slot_ref):
    tokens, width = grad_ref.shape
    experts = slot_ref.shape[0]
    step = pl.program_id(0)
    block_experts = out_ref.shape[0] // SLOTS
    piece = 2 * width // PARTS

    @pl.when(step == 0)
    def _():
        hid = hid_ref[...].astype(F32)
        inv_rms = lax.rsqrt(jnp.mean(hid * hid, axis=1, keepdims=True) + 1e-06)
        normed = (hid * inv_rms * gain_ref[...]).astype(BF)
        grad = grad_ref[...]
        rows_ref[:, :width] = grad
        rows_ref[:, width:] = normed
        half = PARTS // 2
        for part in range(half):
            parts_ref[part * tokens : (part + 1) * tokens, :] = grad[
                :, part * piece : (part + 1) * piece
            ]
            parts_ref[(half + part) * tokens : (half + part + 1) * tokens, :] = normed[
                :, part * piece : (part + 1) * piece
            ]
        slot_ref[...] = routing(ids_ref[...], experts).T

    start = pl.multiple_of(step * block_experts, block_experts)
    slot = per_row(slot_ref[pl.ds(start, block_experts), :])
    place = iota(slot.shape, 0) & (SLOTS - 1)
    pick = jnp.where(slot == place.astype(F32), 1.0, 0.0).astype(BF)
    chunk = 1024
    for col in range(0, 2 * width, chunk):
        out_ref[:, col : col + chunk] = dot_nn(pick, rows_ref[:, col : col + chunk]).astype(BF)
    late = slot == (SLOTS + (place >> 2)).astype(F32)
    pick_late = jnp.concatenate(
        [
            jnp.where(late & ((place & (PARTS - 1)) == part), 1.0, 0.0).astype(BF)
            for part in range(PARTS)
        ],
        axis=1,
    )
    out_ref[:, 2 * width :] = dot_nn(pick_late, parts_ref[...]).astype(BF)


def dispatch(ids, grad_out, hidden_in, gain, experts):
    tokens, width = grad_out.shape
    total = 2 * width + 2 * width // PARTS
    steps = 4
    rows = experts * SLOTS
    return kernel_call(
        dispatch_kernel,
        out_shape=jax.ShapeDtypeStruct((rows, total), BF),
        grid=(steps,),
        in_specs=[
            whole(ids.shape),
            whole(grad_out.shape),
            whole(hidden_in.shape),
            whole(gain.shape),
        ],
        out_specs=pl.BlockSpec((rows // steps, total), lambda i: (i, 0)),
        scratch_shapes=[
            pltpu.VMEM((tokens, 2 * width), BF),
            pltpu.VMEM((PARTS * tokens, 2 * width // PARTS), BF),
            pltpu.VMEM((experts, tokens), F32),
        ],
        vmem=16,
        name="dispatch",
    )(ids, grad_out, hidden_in, gain)


def expert_kernel(
    rows_hbm,
    gate_hbm,
    up_hbm,
    down_hbm,
    out_hbm,
    rows_ref,
    gate_ref,
    up_ref,
    down_ref,
    late_ref,
    act_ref,
    out_ref,
    in_sems,
    out_sems,
):
    width, hidden = gate_ref.shape
    rows = rows_ref.shape[0]
    group = rows // 2
    late = group // SLOTS * EXTRA
    quarter = width // PARTS
    chunk = 256

    def fetch(source, target, n):
        copy = pltpu.make_async_copy(source, target, in_sems.at[n])
        copy.start()
        return copy

    def columns(lo, first, last, n):
        at = (slice(lo, lo + group), slice(first, last))
        return fetch(rows_hbm.at[at], rows_ref.at[at], n)

    norm_0 = columns(0, width, 2 * width, 0)
    gate_in = fetch(gate_hbm, gate_ref, 1)
    up_in = fetch(up_hbm, up_ref, 2)
    grad_0 = columns(0, 0, width, 3)
    down_in = fetch(down_hbm, down_ref, 4)
    all_1 = columns(group, 0, 2 * width, 5)
    late_0 = columns(0, 2 * width, 2 * width + 2 * quarter, 6)
    late_1 = columns(group, 2 * width, 2 * width + 2 * quarter, 7)

    def backward(norm, grad, before_up=(), before_grad=(), acts=None):
        gate_pre = dot_nn(norm(), gate_ref[...])
        for copy in before_up:
            copy.wait()
        up_pre = dot_nn(norm(), up_ref[...])
        for copy in before_grad:
            copy.wait()
        score = None
        for col in range(0, hidden, chunk):
            cols = slice(col, col + chunk)
            grad_hid = dot_nt(grad(), down_ref[cols, :])
            gate_part = gate_pre[:, cols]
            sigma = jax.nn.sigmoid(gate_part)
            act = gate_part * sigma
            slope = sigma * (1.0 + gate_part * (1.0 - sigma))
            grad_up = grad_hid * up_pre[:, cols]
            partial = jnp.sum(grad_up * act, axis=1, keepdims=True)
            score = partial if score is None else score + partial
            acts[:, cols] = (grad_up * slope).astype(BF)
            acts[:, hidden + col : hidden + col + chunk] = (grad_hid * act).astype(BF)
        return score

    def pair(acts, cols):
        total = dot_nt(acts[:, :hidden], gate_ref[cols, :])
        return (total + dot_nt(acts[:, hidden:], up_ref[cols, :])).astype(BF)

    sent = []

    def send(lo, height, first, last):
        at = (slice(lo, lo + height), slice(first, last))
        copy = pltpu.make_async_copy(out_ref.at[at], out_hbm.at[at], out_sems.at[len(sent)])
        copy.start()
        sent.append(copy)

    main_scores = []
    for index in range(2):
        at = slice(index * group, (index + 1) * group)
        if index == 0:
            norm_0.wait()
            gate_in.wait()
            waits = ((up_in,), (grad_0, down_in))
        else:
            all_1.wait()
            waits = ((), ())
        acts = act_ref.at[at]
        main_scores.append(
            backward(
                lambda: rows_ref[at, width : 2 * width], lambda: rows_ref[at, :width], *waits, acts
            )
        )
        for col in range(0, width, quarter):
            cols = slice(col, col + quarter)
            out_ref[at, cols] = pair(acts, cols)
        send(index * group, group, 0, width)

    late_0.wait()
    late_1.wait()
    half = group // 2
    few = half // SLOTS * EXTRA
    order = iota((half, half), 0)
    source = (order % few) * PARTS + order // few
    gather = jnp.where(iota((half, half), 1) == source, 1.0, 0.0).astype(BF)
    for block in range(rows // half):
        moved = dot_nn(gather, rows_ref[block * half : (block + 1) * half, 2 * width :]).astype(BF)
        for part in range(PARTS):
            late_ref[block * few : (block + 1) * few, part * 2 * quarter : (part + 1) * 2 * quarter] = (
                moved[part * few : (part + 1) * few]
            )
    acts = act_ref.at[rows:]
    late_score = backward(
        lambda: late_ref[:, width : 2 * width], lambda: late_ref[:, :width], acts=acts
    )
    ends = [pair(acts, slice(col, col + quarter)) for col in range(0, width, quarter)]
    order = iota((half, half), 1)
    scatter = jnp.where(
        iota((half, half), 0) == (order % few) * PARTS + order // few, 1.0, 0.0
    ).astype(BF)
    spread = jnp.where((iota((half, few), 0) >> 2) == iota((half, few), 1), 1.0, 0.0).astype(BF)
    lane = iota((half, LANES), 1)
    for block in range(rows // half):
        at = slice(block * half, (block + 1) * half)
        own = slice(block * few, (block + 1) * few)
        stacked = jnp.concatenate([end[own] for end in ends], axis=0)
        out_ref[at, width : width + quarter] = dot_nn(scatter, stacked).astype(BF)
        spread_score = dot_nn(spread, jnp.broadcast_to(late_score[own], (few, LANES)).astype(BF))
        start = (block % 2) * half
        main_score = main_scores[block // 2][start : start + half]
        out_ref[at, width + quarter :] = jnp.where(
            lane == 0, main_score, jnp.where(lane == 1, spread_score, 0.0)
        ).astype(BF)
    send(0, rows, width, width + quarter + LANES)
    for copy in sent:
        copy.wait()


def expert_backward(arrived, gate_mat, up_mat, down_mat):
    rows = arrived.shape[0]
    width, hidden = gate_mat.shape
    late = rows // SLOTS * EXTRA
    out_shape = (rows, width + width // PARTS + LANES)
    return kernel_call(
        expert_kernel,
        out_shape=jax.ShapeDtypeStruct(out_shape, BF),
        in_specs=[RAW] * 4,
        out_specs=RAW,
        scratch_shapes=[
            pltpu.VMEM(arrived.shape, BF),
            pltpu.VMEM(gate_mat.shape, BF),
            pltpu.VMEM(up_mat.shape, BF),
            pltpu.VMEM(down_mat.shape, BF),
            pltpu.VMEM((late, 2 * width), BF),
            pltpu.VMEM((rows + late, 2 * hidden), BF),
            pltpu.VMEM(out_shape, BF),
            pltpu.SemaphoreType.DMA((8,)),
            pltpu.SemaphoreType.DMA((3,)),
        ],
        vmem=58,
        name="expert",
    )(arrived, gate_mat, up_mat, down_mat)


def whole(shape):
    return pl.BlockSpec(shape, lambda i: (0,) * len(shape))


def placed(ids, rows):
    experts = rows // SLOTS
    slot = per_row(routing(ids, experts).T)
    place = iota(slot.shape, 0) & (SLOTS - 1)
    return slot == place.astype(F32), slot == (SLOTS + (place >> 2)).astype(F32), place


def plan_kernel(ids_ref, weight_ref, first_ref, late_ref):
    ids = ids_ref[...]
    weights = weight_ref[...]
    tokens, top = ids.shape
    rows = first_ref.shape[1]
    experts = rows // SLOTS
    lane = iota((tokens, experts), 1)
    weight = jnp.zeros((tokens, experts), F32)
    for k in range(top):
        weight = weight + jnp.where(ids[:, k : k + 1] == lane, weights[:, k : k + 1], 0.0)
    weight = per_row(weight.T)
    first, late, place = placed(ids, rows)
    high = weight.astype(BF).astype(F32)
    for n, value in enumerate((high, weight - high)):
        first_ref[n * tokens : (n + 1) * tokens, :] = jnp.where(first, value, 0.0).T.astype(BF)
        for part in range(PARTS):
            start = (2 * part + n) * tokens
            hit = late & ((place & (PARTS - 1)) == part)
            late_ref[start : start + tokens, :] = jnp.where(hit, value, 0.0).T.astype(BF)


def plan(ids, weights, experts):
    tokens = ids.shape[0]
    rows = experts * SLOTS
    return kernel_call(
        plan_kernel,
        out_shape=(
            jax.ShapeDtypeStruct((2 * tokens, rows), BF),
            jax.ShapeDtypeStruct((2 * PARTS * tokens, rows), BF),
        ),
        space=pltpu.VMEM,
        vmem=16,
        name="plan",
    )(ids, weights)


def combine_kernel(
    first_ref,
    late_ref,
    grad_ref,
    hid_ref,
    gain_ref,
    back_hbm,
    proj_hbm,
    out_ref,
    attn_ref,
    back_ref,
    proj_ref,
    sems,
):
    tokens, width = grad_ref.shape
    quarter = width // PARTS
    pieces, owners, piece, _ = proj_ref.shape
    group = owners // 8
    heads = attn_ref.shape[1]

    def fetch(source, target, n):
        copy = pltpu.make_async_copy(source, target, sems.at[n])
        copy.start()
        return copy

    backs = []
    for n, part in enumerate((PARTS,) + tuple(range(PARTS))):
        at = (slice(None), slice(part * quarter, (part + 1) * quarter))
        backs.append(fetch(back_hbm.at[at], back_ref.at[at], n))
    def proj_copy(n):
        at = (slice(None), pl.ds(n * group, group))
        return pltpu.make_async_copy(proj_hbm.at[at], proj_ref.at[at], sems.at[len(backs) + n])

    for n in range(8):
        proj_copy(n).start()

    hid = hid_ref[...].astype(F32)
    inv_rms = lax.rsqrt(jnp.mean(hid * hid, axis=1, keepdims=True) + 1e-06)
    backs[0].wait()
    late = dot_nn(late_ref[...], back_ref[:, width:])
    total = jnp.zeros((tokens, 1), F32)
    parts = []
    for part in range(PARTS):
        cols = slice(part * quarter, (part + 1) * quarter)
        backs[1 + part].wait()
        moe = dot_nn(first_ref[...], back_ref[:, cols])
        begin = 2 * part * tokens
        moe = (moe[:tokens] + moe[tokens:]) + (
            late[begin : begin + tokens] + late[begin + tokens : begin + 2 * tokens]
        )
        scaled = moe * gain_ref[:, cols]
        parts.append(scaled)
        total = total + jnp.sum(scaled * (hid[:, cols] * inv_rms), axis=1, keepdims=True)
    inner_mean = total * (1.0 / width)
    for part in range(PARTS):
        cols = slice(part * quarter, (part + 1) * quarter)
        change = parts[part] - hid[:, cols] * inv_rms * inner_mean
        out_ref[:, cols] = (grad_ref[:, cols].astype(F32) + inv_rms * change).astype(BF)

    def project(n, carry):
        proj_copy(n).wait()
        for index in range(group):
            owner = n * group + index
            proj = proj_ref[:, owner].reshape(pieces * piece, width)
            grad = dot_nt(out_ref[...], proj).astype(BF)
            for head in range(heads):
                attn_ref[owner, head] = grad[:, head * HD : (head + 1) * HD]
        return carry

    lax.fori_loop(0, 8, project, 0)


def combine(first, late, grad_out, hidden_in, gain, back, proj):
    tokens, width = grad_out.shape
    pieces, owners, piece, _ = proj.shape
    heads = pieces * piece // HD
    return kernel_call(
        combine_kernel,
        out_shape=(
            jax.ShapeDtypeStruct(grad_out.shape, BF),
            jax.ShapeDtypeStruct((owners, heads, tokens, HD), BF),
        ),
        in_specs=[HELD] * 5 + [RAW] * 2,
        out_specs=(HELD, HELD),
        scratch_shapes=[
            pltpu.VMEM((back.shape[0], width + width // PARTS), BF),
            pltpu.VMEM(proj.shape, BF),
            pltpu.SemaphoreType.DMA((PARTS + 9,)),
        ],
        vmem=50,
        space=None,
        free=(0, 1, 2, 3, 4),
        name="combine",
    )(first, late, grad_out, hidden_in, gain, back, proj)


def score_kernel(ids_ref, score_ref, gate_ref):
    ids = ids_ref[...]
    tokens, top = ids.shape
    rows = score_ref.shape[0]
    experts = rows // SLOTS
    score = score_ref[...].astype(F32)
    first, late, place = placed(ids, rows)
    got = jnp.where(first, score[:, 0:1], 0.0) + jnp.where(
        late & ((place & (PARTS - 1)) == 0), score[:, 1:2], 0.0
    )
    by_expert = jnp.sum(got.reshape(experts, SLOTS, tokens), axis=1).T
    lane = iota((tokens, experts), 1)
    column = iota((tokens, top), 1)
    gate = jnp.zeros((tokens, top), F32)
    for k in range(top):
        value = jnp.sum(jnp.where(ids[:, k : k + 1] == lane, by_expert, 0.0), axis=1, keepdims=True)
        gate = gate + jnp.where(column == k, value, 0.0)
    gate_ref[...] = gate.astype(BF)


def scores(ids, back):
    rows, total = back.shape
    return kernel_call(
        score_kernel,
        out_shape=jax.ShapeDtypeStruct(ids.shape, BF),
        grid=(1,),
        in_specs=[
            whole(ids.shape),
            pl.BlockSpec((rows, LANES), lambda i: (0, total // LANES - 1)),
        ],
        out_specs=whole(ids.shape),
        vmem=16,
        name="scores",
    )(ids, back)


BLOCK = 256


def probs_kernel(q_ref, k_ref, out_ref):
    length = q_ref.shape[0]
    scale = HD ** (-0.5)
    start = 0
    for lo in range(0, length, BLOCK):
        hi = lo + BLOCK
        scores = dot_nt(k_ref[:hi, :], q_ref[lo:hi, :])
        corner = jnp.where(
            iota((BLOCK, BLOCK), 0) <= iota((BLOCK, BLOCK), 1), scores[lo:], -jnp.inf
        )
        scores = jnp.concatenate([scores[:lo], corner], axis=0) if lo else corner
        peak = jnp.max(scores, axis=0, keepdims=True)
        exp_scores = jnp.exp((scores - peak) * scale)
        total = jnp.sum(exp_scores, axis=0, keepdims=True)
        out_ref[start : start + hi, :] = (exp_scores * (1.0 / total)).astype(BF)
        start += hi


def packed_rows(length):
    return sum(range(BLOCK, length + 1, BLOCK))


def attention_probs(query, key):
    tokens, cols = query.shape
    length = tokens // SEQS
    heads = cols // HD
    item = pl.BlockSpec((length, HD), lambda s, h: (s, h))
    return kernel_call(
        probs_kernel,
        out_shape=jax.ShapeDtypeStruct((SEQS, heads, packed_rows(length), BLOCK), BF),
        grid=(SEQS, heads),
        in_specs=[item, item],
        out_specs=pl.BlockSpec((None, None, packed_rows(length), BLOCK), lambda s, h: (s, h, 0, 0)),
        vmem=16,
        name="probs",
    )(query, key)


def attention_kernel(probs_ref, grad_ref, q_ref, k_ref, v_ref, dq_ref, dk_ref, dv_ref, acc_k, acc_v):
    length = q_ref.shape[0]
    scale = HD ** (-0.5)
    grad_all = grad_ref[...].reshape(length, HD)
    start = 0
    for lo in range(0, length, BLOCK):
        hi = lo + BLOCK
        query = q_ref[lo:hi, :]
        grad = grad_all[lo:hi]
        probs = probs_ref[start : start + hi, :]
        start += hi
        full = probs.astype(F32)
        grad_probs = dot_nt(v_ref[:hi, :], grad)
        delta = jnp.sum(full * grad_probs, axis=0, keepdims=True)
        grad_scores = (full * (grad_probs - delta)).astype(BF)
        dq_ref[lo:hi, :] = (scale * dot_tn(grad_scores, k_ref[:hi, :])).astype(BF)
        dv = dot_nn(probs, grad)
        dk = dot_nn(grad_scores, query)
        if lo:
            acc_k[:lo, :] += dk[:lo]
            acc_v[:lo, :] += dv[:lo]
        acc_k[lo:hi, :] = dk[lo:]
        acc_v[lo:hi, :] = dv[lo:]
    dk_ref[...] = (scale * acc_k[...]).astype(BF)
    dv_ref[...] = acc_v[...].astype(BF)


def attention(probs, grad_attn, query, key, value):
    tokens, cols = query.shape
    length = tokens // SEQS
    owners, _, part, _ = grad_attn.shape
    item = pl.BlockSpec((length, HD), lambda s, h: (s, h))
    return kernel_call(
        attention_kernel,
        out_shape=[jax.ShapeDtypeStruct(query.shape, BF)] * 3,
        grid=(SEQS, cols // HD),
        in_specs=[
            pl.BlockSpec((None, None) + probs.shape[2:], lambda s, h: (s, h, 0, 0)),
            pl.BlockSpec((owners // SEQS, None, part, HD), lambda s, h: (s, h, 0, 0)),
            item,
            item,
            item,
        ],
        out_specs=[item] * 3,
        scratch_shapes=[pltpu.VMEM((length, HD), F32), pltpu.VMEM((length, HD), F32)],
        vmem=24,
        free=(1,),
        name="attention",
    )(probs, grad_attn, query, key, value)


def exchange(rows, experts):
    total = rows.shape[1]
    moved = lax.all_to_all(
        rows.reshape(experts, SLOTS, total),
        ("group", "inner"),
        split_axis=0,
        concat_axis=0,
        tiled=True,
    )
    return moved.reshape(experts * SLOTS, total)


def local(
    grad_out,
    hidden_in,
    norm_gain,
    expert_ids,
    gate_weights,
    gate_proj,
    up_proj,
    down_proj,
    out_proj,
    query_rows,
    key_rows,
    value_rows,
):
    groups = lax.axis_size("group")
    owners = lax.axis_size("inner")
    experts = groups * owners
    gain = norm_gain.reshape(1, -1)
    tokens, width = grad_out.shape
    piece = out_proj.shape[0] // groups
    own_proj = lax.dynamic_slice_in_dim(out_proj, lax.axis_index("group") * piece, piece, 0)
    proj = lax.all_gather(own_proj, ("group", "inner"), axis=0, tiled=False)
    outgoing = dispatch(expert_ids, grad_out, hidden_in, gain, experts)
    outgoing, query = lax.optimization_barrier((outgoing, query_rows))
    arrived = exchange(outgoing, experts)
    probs = attention_probs(query, key_rows)
    arrived, probs = lax.optimization_barrier((arrived, probs))
    answers = expert_backward(arrived, gate_proj[0], up_proj[0], down_proj[0])
    answers, ids = lax.optimization_barrier((answers, expert_ids))
    back = exchange(answers, experts)
    first, late = plan(ids, gate_weights, experts)
    back, first, late = lax.optimization_barrier((back, first, late))
    grad_hidden, grad_attn = combine(
        first, late, grad_out, hidden_in, gain, back, proj.reshape(groups, owners, piece, width)
    )
    heads = grad_attn.shape[1]
    grad_attn, back = lax.optimization_barrier((grad_attn, back))
    grad_gate = scores(expert_ids, back)
    grad_attn = lax.all_to_all(
        grad_attn.reshape(owners, heads * tokens, HD),
        "inner",
        split_axis=0,
        concat_axis=0,
        tiled=True,
    )
    grad_attn, grad_gate = lax.optimization_barrier((grad_attn, grad_gate))
    grad_q, grad_k, grad_v = attention(
        probs, grad_attn.reshape(owners, heads, tokens, HD), query_rows, key_rows, value_rows
    )
    return (grad_hidden, grad_gate, grad_q, grad_k, grad_v)


def solution(mesh):
    rows = P(("group", "inner"), None)
    stack = P(("group", "inner"), None, None)
    heads = P("group", "inner")
    return jax.shard_map(
        local,
        mesh=mesh,
        in_specs=(
            rows,
            rows,
            P(),
            rows,
            rows,
            stack,
            stack,
            stack,
            P("inner", None),
            heads,
            heads,
            heads,
        ),
        out_specs=(rows, rows, heads, heads, heads),
        check_vma=False,
    )
```

time: 347 us -> 327 us (0.942)
  local copies, waits for them, and re-layouts: 19.2 us -> 7.47 us
  waiting for transfers between devices: 208 us -> 202 us
    unnamed x35 -> x19, local copies, waits for them, and re-layouts: 18.5 us -> 6.08 us
    all_to_all x2, waiting for transfers between devices: 190 us -> 186 us  [exchange(): lax.all_to_all(rows.reshape(experts, SLOTS, total), ('group', 'inner'), s...]
    pallas_call x5 -> x7, Pallas kernels: 75.7 us -> 75.6 us  [kernel_call(): call(*[arg if n in free else pin(arg) for n, arg in enumerate(args)])]
  transfers between devices with their start and end apart: 4 -> 4, of which waited for: 3 -> 3; matrix products, arithmetic and copies ran while one was open for 0% -> 1% of each run, Pallas kernels for 14% -> 15%
where the time goes in v3:
time: 327 us
  waiting for transfers between devices  202 us (62%)
  Pallas kernels  75.6 us (23%)
  starting transfers between devices  28 us (9%)
  between operations  14.2 us (4%)
  local copies, waits for them, and re-layouts  7.47 us (2%)
    all_to_all x2, waiting for transfers between devices, exchange(): lax.all_to_all(rows.reshape(experts, SLOTS, total), ('group', 'inner'), s...  186 us
    pallas_call x7, Pallas kernels, kernel_call(): call(*[arg if n in free else pin(arg) for n, arg in enumerate(args)])  75.6 us
    all_to_all x2, starting transfers between devices, exchange(): lax.all_to_all(rows.reshape(experts, SLOTS, total), ('group', 'inner'), s...  24 us
    all_to_all x1, waiting for transfers between devices, local(): lax.all_to_all(grad_attn.reshape(owners, heads * tokens, HD), 'inner', sp...  15.3 us
  transfers between devices with their start and end apart: 4, of which 3 were waited for; matrix products, arithmetic and copies ran while one was open for 1% of the time, Pallas kernels for 15%

profile of v3, /device:TPU:0, one launch (start us, length us, event | category | flops | bytes accessed | tf_op | source)
XLA Modules:
  0.0 326.8 jit_solution(16560765688175267411)
XLA Ops:
  7.2 0.0 copy-start
  7.2 0.0 all-gather.3.cloned.1.call-start
  7.2 1.2 copy-done
  8.4 0.7 constant_dynamic-slice_fusion
  9.1 0.0 all-gather.3.cloned.1.call-update
  9.1 1.4 copy.17.ids_ref
  10.5 8.0 %dispatch.1 = bf16[1024,5120]{1,0:T(8,128)(2,1)} custom-call(s32[128,8]{1,0:T(8,128)} %copy.17.ids_ref, bf16[128,2048]{1,0:T(8,128)(2,1)} %grad_ref.3, bf16[128,2048]{1,0:T(8,128)(2,1)} %hid_ref.3, f32[1,2048]{1,0:T(1,128)} %bitcast.12), custom_call_target="tpu_custom_call" | custom-call | tf_op jit(solution)/shard_map/dispatch/pallas_call | solution.py:47
  18.5 11.6 %all-to-all-start = ((bf16[128,8,5120]{2,1,0:T(8,128)(2,1)}), bf16[128,8,5120]{2,1,0:T(8,128)(2,1)}, u32[]{:S(2)}, u32[]{:S(2)}) async-start(bf16[128,8,5120]{2,1,0:T(8,128)(2,1)} %bitcast.14), calls=%async_computation | async-start | bytes 20971520 | tf_op jit(solution)/shard_map/all_to_all | solution.py:576
  30.1 7.0 %probs.1.probs_ref = bf16[2,2,2560,256]{3,2,1,0:T(8,128)(2,1)} custom-call(bf16[2048,256]{1,0:T(8,128)(2,1)} %q_ref.2, bf16[2048,256]{1,0:T(8,128)(2,1)} %k_ref.3), custom_call_target="tpu_custom_call" | custom-call | tf_op jit(solution)/shard_map/probs/pallas_call | solution.py:47
  37.1 125.7 %all-to-all-done = bf16[128,8,5120]{2,1,0:T(8,128)(2,1)} async-done(((bf16[128,8,5120]{2,1,0:T(8,128)(2,1)}), bf16[128,8,5120]{2,1,0:T(8,128)(2,1)}, u32[]{:S(2)}, u32[]{:S(2)}) %all-to-all-start) | async-done | bytes 10485792 | tf_op jit(solution)/shard_map/all_to_all | solution.py:576
  162.7 29.3 %expert.1 = bf16[1024,2688]{1,0:T(8,128)(2,1)} custom-call(bf16[1024,5120]{1,0:T(8,128)(2,1)} %bitcast.2.rows_hbm, bf16[2048,768]{1,0:T(8,128)(2,1)} %bitcast.17, bf16[2048,768]{1,0:T(8,128)(2,1)} %bitcast.18, bf16[768,2048]{1,0:T(8,128)(2,1)} %bitcast.19), custom_call_target="tpu_custom_call" | custom-call | tf_op jit(solution)/shard_map/expert/pallas_call | solution.py:47
  192.1 0.0 copy-start.7
  192.1 0.0 copy-start.6
  192.1 0.0 copy-start.3
  192.1 0.0 copy-start.4
  192.1 0.0 copy-start.5
  192.2 12.4 %all-to-all-start.1 = ((bf16[128,8,2688]{2,1,0:T(8,128)(2,1)}), bf16[128,8,2688]{2,1,0:T(8,128)(2,1)}, u32[]{:S(2)}, u32[]{:S(2)}) async-start(bf16[128,8,2688]{2,1,0:T(8,128)(2,1)} %bitcast.15), calls=%async_computation.1 | async-start | bytes 11010048 | tf_op jit(solution)/shard_map/all_to_all | solution.py:576
  204.6 0.0 copy-done.7
  204.6 0.7 copy.19.weight_ref
  205.3 0.0 copy-done.6
  205.3 0.7 copy.18.ids_ref
  206.1 2.6 plan.1
  208.6 1.3 copy-done.2
  209.9 60.5 %all-to-all-done.1 = bf16[128,8,2688]{2,1,0:T(8,128)(2,1)} async-done(((bf16[128,8,2688]{2,1,0:T(8,128)(2,1)}), bf16[128,8,2688]{2,1,0:T(8,128)(2,1)}, u32[]{:S(2)}, u32[]{:S(2)}) %all-to-all-start.1) | async-done | bytes 5505056 | tf_op jit(solution)/shard_map/all_to_all | solution.py:576
  270.5 14.0 %combine.1 = (bf16[128,2048]{1,0:T(8,128)(2,1)}, bf16[16,2,128,128]{3,2,1,0:T(8,128)(2,1)}) custom-call(bf16[256,1024]{1,0:T(8,128)(2,1)S(1)} %get-tuple-element.32.first_ref, bf16[1024,1024]{1,0:T(8,128)(2,1)} %copy-done.2, bf16[128,2048]{1,0:T(8,128)(2,1)S(1)} %copy-done.3, bf16[128,2048]{1,0:T(8,128)(2,1)S(1)} %copy-done.4, f32[1,2048]{1,0:T(1,128)S(1)} %bitcast.13, ...), custom_call_target="tpu_custom_call" | custom-call | tf_op jit(solution)/shard_map/combine/pallas_call | solution.py:47
  284.4 3.9 %all-to-all-start.2 = ((bf16[16,256,128]{2,1,0:T(8,128)(2,1)}), bf16[16,256,128]{2,1,0:T(8,128)(2,1)S(1)}, u32[]{:S(2)}, u32[]{:S(2)}) async-start(bf16[16,256,128]{2,1,0:T(8,128)(2,1)} %bitcast.9), calls=%async_computation.2 | async-start | bytes 2097152 | tf_op jit(solution)/shard_map/all_to_all | solution.py:624
  288.4 0.0 copy-start.1
  288.4 2.7 scores.1
  291.1 15.3 %all-to-all-done.2 = bf16[16,256,128]{2,1,0:T(8,128)(2,1)S(1)} async-done(((bf16[16,256,128]{2,1,0:T(8,128)(2,1)}), bf16[16,256,128]{2,1,0:T(8,128)(2,1)S(1)}, u32[]{:S(2)}, u32[]{:S(2)}) %all-to-all-start.2) | async-done | bytes 1048608 | tf_op jit(solution)/shard_map/all_to_all | solution.py:624
  306.4 1.4 copy.21
  307.9 12.1 %attention.1 = (bf16[2048,256]{1,0:T(8,128)(2,1)}, bf16[2048,256]{1,0:T(8,128)(2,1)}, bf16[2048,256]{1,0:T(8,128)(2,1)}) custom-call(bf16[2,2,2560,256]{3,2,1,0:T(8,128)(2,1)} %probs.1.probs_ref, bf16[16,2,128,128]{3,2,1,0:T(8,128)(2,1)S(1)} %bitcast.11, bf16[2048,256]{1,0:T(8,128)(2,1)} %q_ref.2, bf16[2048,256]{1,0:T(8,128)(2,1)} %k_ref.3, ...), custom_call_target="tpu_custom_call" | custom-call | tf_op jit(solution)/shard_map/attention/pallas_call | solution.py:47
  319.9 0.0 copy-done.1
  (5 shorter events, 0.0 us)
Async XLA Ops:
  7.2 1.2 copy-start
  7.2 263.3 %all-gather.3.cloned.1.call-start = ((), (), s32[]{:S(2)}) async-start(), calls=%async_computation.3 | async-start | bytes 16908288 | tf_op jit(solution)/shard_map/all_gather | solution.py:607
  18.5 144.3 %all-to-all-start = ((bf16[128,8,5120]{2,1,0:T(8,128)(2,1)}), bf16[128,8,5120]{2,1,0:T(8,128)(2,1)}, u32[]{:S(2)}, u32[]{:S(2)}) async-start(bf16[128,8,5120]{2,1,0:T(8,128)(2,1)} %bitcast.14), calls=%async_computation | async-start | bytes 20971520 | tf_op jit(solution)/shard_map/all_to_all | solution.py:576
  192.1 12.5 %copy-start.7 = (f32[128,8]{0,1:T(8,128)S(1)}, f32[128,8]{0,1:T(8,128)}, u32[]{:S(2)}) copy-start(f32[128,8]{0,1:T(8,128)} %param.16) | copy-start | bytes 12292
  192.1 13.2 %copy-start.6 = (s32[128,8]{0,1:T(8,128)S(1)}, s32[128,8]{0,1:T(8,128)}, u32[]{:S(2)}) copy-start(s32[128,8]{0,1:T(8,128)} %param.15) | copy-start | bytes 12292
  192.1 78.3 %copy-start.3 = (bf16[128,2048]{1,0:T(8,128)(2,1)S(1)}, bf16[128,2048]{1,0:T(8,128)(2,1)}, u32[]{:S(2)}) copy-start(bf16[128,2048]{1,0:T(8,128)(2,1)} %grad_ref.3) | copy-start | bytes 1572868
  192.1 78.3 %copy-start.4 = (bf16[128,2048]{1,0:T(8,128)(2,1)S(1)}, bf16[128,2048]{1,0:T(8,128)(2,1)}, u32[]{:S(2)}) copy-start(bf16[128,2048]{1,0:T(8,128)(2,1)} %hid_ref.3) | copy-start | bytes 1572868
  192.1 78.3 %copy-start.5 = (f32[2048]{0:T(1024)S(1)}, f32[2048]{0:T(1024)}, u32[]{:S(2)}) copy-start(f32[2048]{0:T(1024)} %param.14) | copy-start | bytes 24580
  192.2 78.3 %all-to-all-start.1 = ((bf16[128,8,2688]{2,1,0:T(8,128)(2,1)}), bf16[128,8,2688]{2,1,0:T(8,128)(2,1)}, u32[]{:S(2)}, u32[]{:S(2)}) async-start(bf16[128,8,2688]{2,1,0:T(8,128)(2,1)} %bitcast.15), calls=%async_computation.1 | async-start | bytes 11010048 | tf_op jit(solution)/shard_map/all_to_all | solution.py:576
  208.6 1.3 copy-start.2
  284.4 22.0 %all-to-all-start.2 = ((bf16[16,256,128]{2,1,0:T(8,128)(2,1)}), bf16[16,256,128]{2,1,0:T(8,128)(2,1)S(1)}, u32[]{:S(2)}, u32[]{:S(2)}) async-start(bf16[16,256,128]{2,1,0:T(8,128)(2,1)} %bitcast.9), calls=%async_computation.2 | async-start | bytes 2097152 | tf_op jit(solution)/shard_map/all_to_all | solution.py:624
  288.4 31.6 %copy-start.1 = (bf16[256,2048]{1,0:T(8,128)(2,1)S(1)}, bf16[256,2048]{1,0:T(8,128)(2,1)}, u32[]{:S(2)}) copy-start(bf16[256,2048]{1,0:T(8,128)(2,1)} %param.20) | copy-start | bytes 3145732
Sparse Core Ops, SparseCore 0:
  11.7 189.1 all-gather.2

commit v4 on v3

--- a/solution.py
+++ b/solution.py
@@ -47,18 +47,22 @@
     return lambda *args: call(*[arg if n in free else pin(arg) for n, arg in enumerate(args)])
 
 
+def whole(shape):
+    return pl.BlockSpec(shape, lambda i: (0,) * len(shape))
+
+
 def iota(shape, dim):
     return lax.broadcasted_iota(jnp.int32, shape, dim)
 
 
 def routing(ids, experts):
-    tokens, top = ids.shape
-    lane = iota((tokens, experts), 1)
-    member = jnp.zeros((tokens, experts), F32)
+    top, tokens = ids.shape
+    row = iota((experts, tokens), 0)
+    member = jnp.zeros((experts, tokens), F32)
     for k in range(top):
-        member = member + jnp.where(ids[:, k : k + 1] == lane, 1.0, 0.0)
-    earlier = jnp.where(iota((tokens, tokens), 1) < iota((tokens, tokens), 0), 1.0, 0.0).astype(BF)
-    slot = dot_nn(earlier, member.astype(BF))
+        member = member + jnp.where(ids[k : k + 1, :] == row, 1.0, 0.0)
+    earlier = jnp.where(iota((tokens, tokens), 0) < iota((tokens, tokens), 1), 1.0, 0.0).astype(BF)
+    slot = dot_nn(member.astype(BF), earlier)
     return jnp.where(member > 0.5, slot, -1.0)
 
 
@@ -67,6 +71,27 @@
     return jnp.broadcast_to(by_expert[:, None, :], (experts, SLOTS, width)).reshape(
         experts * SLOTS, width
     )
+
+
+def own_rows_kernel(place_ref, proj_hbm, own_hbm, sem):
+    piece = own_hbm.shape[0]
+    begin = pl.multiple_of(place_ref[0] * piece, piece)
+    own = pltpu.make_async_copy(proj_hbm.at[pl.ds(begin, piece)], own_hbm, sem)
+    own.start()
+    own.wait()
+
+
+def own_rows(place, proj, pieces):
+    return kernel_call(
+        own_rows_kernel,
+        out_shape=jax.ShapeDtypeStruct((proj.shape[0] // pieces, proj.shape[1]), BF),
+        in_specs=[pl.BlockSpec(memory_space=pltpu.SMEM), RAW],
+        out_specs=RAW,
+        scratch_shapes=[pltpu.SemaphoreType.DMA(())],
+        vmem=16,
+        free=(0,),
+        name="own_rows",
+    )(place, proj)
 
 
 def dispatch_kernel(ids_ref, grad_ref, hid_ref, gain_ref, out_ref, rows_ref, parts_ref, slot_ref):
@@ -92,7 +117,7 @@
             parts_ref[(half + part) * tokens : (half + part + 1) * tokens, :] = normed[
                 :, part * piece : (part + 1) * piece
             ]
-        slot_ref[...] = routing(ids_ref[...], experts).T
+        slot_ref[...] = routing(ids_ref[...], experts)
 
     start = pl.multiple_of(step * block_experts, block_experts)
     slot = per_row(slot_ref[pl.ds(start, block_experts), :])
@@ -134,6 +159,7 @@
             pltpu.VMEM((experts, tokens), F32),
         ],
         vmem=16,
+        space=None,
         name="dispatch",
     )(ids, grad_out, hidden_in, gain)
 
@@ -295,18 +321,14 @@
             pltpu.SemaphoreType.DMA((8,)),
             pltpu.SemaphoreType.DMA((3,)),
         ],
-        vmem=58,
+        vmem=48,
         name="expert",
     )(arrived, gate_mat, up_mat, down_mat)
 
 
-def whole(shape):
-    return pl.BlockSpec(shape, lambda i: (0,) * len(shape))
-
-
 def placed(ids, rows):
     experts = rows // SLOTS
-    slot = per_row(routing(ids, experts).T)
+    slot = per_row(routing(ids, experts))
     place = iota(slot.shape, 0) & (SLOTS - 1)
     return slot == place.astype(F32), slot == (SLOTS + (place >> 2)).astype(F32), place
 
@@ -314,14 +336,14 @@
 def plan_kernel(ids_ref, weight_ref, first_ref, late_ref):
     ids = ids_ref[...]
     weights = weight_ref[...]
-    tokens, top = ids.shape
+    top, tokens = ids.shape
     rows = first_ref.shape[1]
     experts = rows // SLOTS
-    lane = iota((tokens, experts), 1)
-    weight = jnp.zeros((tokens, experts), F32)
+    row = iota((experts, tokens), 0)
+    weight = jnp.zeros((experts, tokens), F32)
     for k in range(top):
-        weight = weight + jnp.where(ids[:, k : k + 1] == lane, weights[:, k : k + 1], 0.0)
-    weight = per_row(weight.T)
+        weight = weight + jnp.where(ids[k : k + 1, :] == row, weights[k : k + 1, :], 0.0)
+    weight = per_row(weight)
     first, late, place = placed(ids, rows)
     high = weight.astype(BF).astype(F32)
     for n, value in enumerate((high, weight - high)):
@@ -333,7 +355,7 @@
 
 
 def plan(ids, weights, experts):
-    tokens = ids.shape[0]
+    tokens = ids.shape[1]
     rows = experts * SLOTS
     return kernel_call(
         plan_kernel,
@@ -445,7 +467,7 @@
 
 def score_kernel(ids_ref, score_ref, gate_ref):
     ids = ids_ref[...]
-    tokens, top = ids.shape
+    top, tokens = ids.shape
     rows = score_ref.shape[0]
     experts = rows // SLOTS
     score = score_ref[...].astype(F32)
@@ -453,14 +475,13 @@
     got = jnp.where(first, score[:, 0:1], 0.0) + jnp.where(
         late & ((place & (PARTS - 1)) == 0), score[:, 1:2], 0.0
     )
-    by_expert = jnp.sum(got.reshape(experts, SLOTS, tokens), axis=1).T
-    lane = iota((tokens, experts), 1)
-    column = iota((tokens, top), 1)
-    gate = jnp.zeros((tokens, top), F32)
-    for k in range(top):
-        value = jnp.sum(jnp.where(ids[:, k : k + 1] == lane, by_expert, 0.0), axis=1, keepdims=True)
-        gate = gate + jnp.where(column == k, value, 0.0)
-    gate_ref[...] = gate.astype(BF)
+    by_expert = jnp.sum(got.reshape(experts, SLOTS, tokens), axis=1)
+    row = iota((experts, tokens), 0)
+    gates = [
+        jnp.sum(jnp.where(ids[k : k + 1, :] == row, by_expert, 0.0), axis=0, keepdims=True)
+        for k in range(top)
+    ]
+    gate_ref[...] = jnp.concatenate(gates, axis=0).astype(BF)
 
 
 def scores(ids, back):
@@ -482,7 +503,7 @@
 BLOCK = 256
 
 
-def probs_kernel(q_ref, k_ref, out_ref):
+def probs_kernel(q_ref, k_ref, v_ref, out_ref, mixed_ref):
     length = q_ref.shape[0]
     scale = HD ** (-0.5)
     start = 0
@@ -496,7 +517,9 @@
         peak = jnp.max(scores, axis=0, keepdims=True)
         exp_scores = jnp.exp((scores - peak) * scale)
         total = jnp.sum(exp_scores, axis=0, keepdims=True)
-        out_ref[start : start + hi, :] = (exp_scores * (1.0 / total)).astype(BF)
+        probs = (exp_scores * (1.0 / total)).astype(BF)
+        out_ref[start : start + hi, :] = probs
+        mixed_ref[lo:hi, :] = dot_tn(probs, v_ref[:hi, :])
         start += hi
 
 
@@ -504,40 +527,59 @@
     return sum(range(BLOCK, length + 1, BLOCK))
 
 
-def attention_probs(query, key):
+def attention_probs(query, key, value):
     tokens, cols = query.shape
     length = tokens // SEQS
     heads = cols // HD
     item = pl.BlockSpec((length, HD), lambda s, h: (s, h))
+    rows = packed_rows(length)
     return kernel_call(
         probs_kernel,
-        out_shape=jax.ShapeDtypeStruct((SEQS, heads, packed_rows(length), BLOCK), BF),
+        out_shape=(
+            jax.ShapeDtypeStruct((SEQS, heads, rows, BLOCK), BF),
+            jax.ShapeDtypeStruct(query.shape, F32),
+        ),
         grid=(SEQS, heads),
-        in_specs=[item, item],
-        out_specs=pl.BlockSpec((None, None, packed_rows(length), BLOCK), lambda s, h: (s, h, 0, 0)),
-        vmem=16,
+        in_specs=[item] * 3,
+        out_specs=(pl.BlockSpec((None, None, rows, BLOCK), lambda s, h: (s, h, 0, 0)), item),
+        vmem=20,
         name="probs",
-    )(query, key)
-
-
-def attention_kernel(probs_ref, grad_ref, q_ref, k_ref, v_ref, dq_ref, dk_ref, dv_ref, acc_k, acc_v):
+    )(query, key, value)
+
+
+def attention_kernel(
+    probs_ref, mixed_ref, grad_ref, q_ref, k_ref, v_ref, dq_ref, dk_ref, dv_ref, acc_k, acc_v
+):
     length = q_ref.shape[0]
     scale = HD ** (-0.5)
     grad_all = grad_ref[...].reshape(length, HD)
-    start = 0
-    for lo in range(0, length, BLOCK):
-        hi = lo + BLOCK
-        query = q_ref[lo:hi, :]
-        grad = grad_all[lo:hi]
-        probs = probs_ref[start : start + hi, :]
-        start += hi
-        full = probs.astype(F32)
-        grad_probs = dot_nt(v_ref[:hi, :], grad)
-        delta = jnp.sum(full * grad_probs, axis=0, keepdims=True)
-        grad_scores = (full * (grad_probs - delta)).astype(BF)
-        dq_ref[lo:hi, :] = (scale * dot_tn(grad_scores, k_ref[:hi, :])).astype(BF)
-        dv = dot_nn(probs, grad)
-        dk = dot_nn(grad_scores, query)
+    less = -jnp.sum(grad_all.astype(F32) * mixed_ref[...], axis=1, keepdims=True)
+    high = less.astype(BF).astype(F32)
+    mid = (less - high).astype(BF).astype(F32)
+    low = less - high - mid
+    lane = iota((length, HD), 1)
+    extra = jnp.where(lane == 0, high, jnp.where(lane == 1, mid, jnp.where(lane == 2, low, 0.0)))
+    grad_less = jnp.concatenate([grad_all, extra.astype(BF)], axis=1)
+    ones = jnp.where(lane < 3, 1.0, 0.0).astype(BF)
+    values = jnp.concatenate([v_ref[...], ones], axis=1)
+    keys = k_ref[...].T
+    starts = [BLOCK * n * (n + 1) // 2 for n in range(length // BLOCK)]
+
+    def score_grads(n):
+        hi = (n + 1) * BLOCK
+        shifted = dot_nt(values[:hi], grad_less[hi - BLOCK : hi])
+        probs = probs_ref[starts[n] : starts[n] + hi, :]
+        return (probs.astype(F32) * shifted).astype(BF)
+
+    ready = score_grads(0)
+    for n in range(length // BLOCK):
+        lo, hi = n * BLOCK, (n + 1) * BLOCK
+        grad_scores = ready
+        if hi < length:
+            ready = score_grads(n + 1)
+        dq_ref[lo:hi, :] = (scale * dot_nn(keys[:, :hi], grad_scores)).T.astype(BF)
+        dv = dot_nn(probs_ref[starts[n] : starts[n] + hi, :], grad_all[lo:hi])
+        dk = dot_nn(grad_scores, q_ref[lo:hi, :])
         if lo:
             acc_k[:lo, :] += dk[:lo]
             acc_v[:lo, :] += dv[:lo]
@@ -547,7 +589,7 @@
     dv_ref[...] = acc_v[...].astype(BF)
 
 
-def attention(probs, grad_attn, query, key, value):
+def attention(probs, mixed, grad_attn, query, key, value):
     tokens, cols = query.shape
     length = tokens // SEQS
     owners, _, part, _ = grad_attn.shape
@@ -558,6 +600,7 @@
         grid=(SEQS, cols // HD),
         in_specs=[
             pl.BlockSpec((None, None) + probs.shape[2:], lambda s, h: (s, h, 0, 0)),
+            item,
             pl.BlockSpec((owners // SEQS, None, part, HD), lambda s, h: (s, h, 0, 0)),
             item,
             item,
@@ -566,9 +609,9 @@
         out_specs=[item] * 3,
         scratch_shapes=[pltpu.VMEM((length, HD), F32), pltpu.VMEM((length, HD), F32)],
         vmem=24,
-        free=(1,),
+        free=(2,),
         name="attention",
-    )(probs, grad_attn, query, key, value)
+    )(probs, mixed, grad_attn, query, key, value)
 
 
 def exchange(rows, experts):
@@ -603,24 +646,26 @@
     gain = norm_gain.reshape(1, -1)
     tokens, width = grad_out.shape
     piece = out_proj.shape[0] // groups
-    own_proj = lax.dynamic_slice_in_dim(out_proj, lax.axis_index("group") * piece, piece, 0)
+    ids = expert_ids.T
+    own_proj = own_rows(lax.axis_index("group").reshape(1), out_proj, groups)
+    own_proj, ids, grad_now, hidden_now = lax.optimization_barrier(
+        (own_proj, ids, grad_out, hidden_in)
+    )
     proj = lax.all_gather(own_proj, ("group", "inner"), axis=0, tiled=False)
-    outgoing = dispatch(expert_ids, grad_out, hidden_in, gain, experts)
-    outgoing, query = lax.optimization_barrier((outgoing, query_rows))
+    outgoing = dispatch(ids, grad_now, hidden_now, gain, experts)
     arrived = exchange(outgoing, experts)
-    probs = attention_probs(query, key_rows)
-    arrived, probs = lax.optimization_barrier((arrived, probs))
     answers = expert_backward(arrived, gate_proj[0], up_proj[0], down_proj[0])
-    answers, ids = lax.optimization_barrier((answers, expert_ids))
+    answers, ids_late, query = lax.optimization_barrier((answers, ids, query_rows))
     back = exchange(answers, experts)
-    first, late = plan(ids, gate_weights, experts)
-    back, first, late = lax.optimization_barrier((back, first, late))
+    probs, mixed = attention_probs(query, key_rows, value_rows)
+    first, late = plan(ids_late, gate_weights.T, experts)
+    back, probs, mixed, first, late = lax.optimization_barrier((back, probs, mixed, first, late))
     grad_hidden, grad_attn = combine(
         first, late, grad_out, hidden_in, gain, back, proj.reshape(groups, owners, piece, width)
     )
     heads = grad_attn.shape[1]
     grad_attn, back = lax.optimization_barrier((grad_attn, back))
-    grad_gate = scores(expert_ids, back)
+    grad_gate = scores(ids, back).T
     grad_attn = lax.all_to_all(
         grad_attn.reshape(owners, heads * tokens, HD),
         "inner",
@@ -630,7 +675,12 @@
     )
     grad_attn, grad_gate = lax.optimization_barrier((grad_attn, grad_gate))
     grad_q, grad_k, grad_v = attention(
-        probs, grad_attn.reshape(owners, heads, tokens, HD), query_rows, key_rows, value_rows
+        probs,
+        mixed,
+        grad_attn.reshape(owners, heads, tokens, HD),
+        query_rows,
+        key_rows,
+        value_rows,
     )
     return (grad_hidden, grad_gate, grad_q, grad_k, grad_v)
 

time: 327 us -> 308 us (0.942)
  blocking collectives: 0 us -> 137 us
  waiting for transfers between devices: 202 us -> 68.5 us
  starting transfers between devices: 28 us -> 10 us
  local copies, waits for them, and re-layouts: 7.47 us -> 1.41 us
    all_to_all x0 -> x1, blocking collectives: none -> 137 us  [exchange(): lax.all_to_all(rows.reshape(experts, SLOTS, total), ('group', 'inner'), s...]
    all_to_all x2 -> x1, waiting for transfers between devices: 186 us -> 52.5 us  [exchange(): lax.all_to_all(rows.reshape(experts, SLOTS, total), ('group', 'inner'), s...]
    all_to_all x2 -> x1, starting transfers between devices: 24 us -> 6.17 us  [exchange(): lax.all_to_all(rows.reshape(experts, SLOTS, total), ('group', 'inner'), s...]
    unnamed x19 -> x8, local copies, waits for them, and re-layouts: 6.08 us -> 1.41 us
    pallas_call x7 -> x8, Pallas kernels: 75.6 us -> 76.9 us  [kernel_call(): call(*[arg if n in free else pin(arg) for n, arg in enumerate(args)])]
  transfers between devices with their start and end apart: 4 -> 3, of which waited for: 3 -> 2; matrix products, arithmetic and copies ran while one was open for 1% -> 0% of each run, Pallas kernels for 15% -> 16%
where the time goes in v4:
time: 308 us; the launch traced here: 307 us
  blocking collectives  137 us (44%)
  Pallas kernels  76.9 us (25%)
  waiting for transfers between devices  68.5 us (22%)
  between operations  14.1 us (5%)
  starting transfers between devices  10 us (3%)
    all_to_all x1, blocking collectives, exchange(): lax.all_to_all(rows.reshape(experts, SLOTS, total), ('group', 'inner'), s...  137 us
    pallas_call x8, Pallas kernels, kernel_call(): call(*[arg if n in free else pin(arg) for n, arg in enumerate(args)])  76.9 us
    all_to_all x1, waiting for transfers between devices, exchange(): lax.all_to_all(rows.reshape(experts, SLOTS, total), ('group', 'inner'), s...  52.5 us
    all_to_all x1, waiting for transfers between devices, local(): lax.all_to_all(grad_attn.reshape(owners, heads * tokens, HD), 'inner', sp...  16 us
    all_to_all x1, starting transfers between devices, exchange(): lax.all_to_all(rows.reshape(experts, SLOTS, total), ('group', 'inner'), s...  6.17 us
  transfers between devices with their start and end apart: 3, of which 2 were waited for; matrix products, arithmetic and copies ran while one was open for 0% of the time, Pallas kernels for 16%

profile of v4, /device:TPU:0, one launch (start us, length us, event | category | flops | bytes accessed | tf_op | source)
XLA Modules:
  0.0 307.5 jit_solution(95204564288940619)
XLA Ops:
  7.2 0.0 all-gather.3.cloned.1.call-start
  7.2 5.1 %own_rows.1 = bf16[32,2048]{1,0:T(8,128)(2,1)} custom-call(s32[1]{0:T(128)} %bitcast.place_ref, bf16[256,2048]{1,0:T(8,128)(2,1)} %proj_hbm.1), custom_call_target="tpu_custom_call" | custom-call | tf_op jit(solution)/shard_map/own_rows/pallas_call | solution.py:47
  12.3 0.0 all-gather.3.cloned.1.call-update
  12.3 5.5 %dispatch.1 = bf16[1024,5120]{1,0:T(8,128)(2,1)S(1)} custom-call(s32[8,128]{1,0:T(8,128)} %bitcast.25, bf16[128,2048]{1,0:T(8,128)(2,1)} %grad_ref.2, bf16[128,2048]{1,0:T(8,128)(2,1)} %hid_ref.2, f32[1,2048]{1,0:T(1,128)} %bitcast.17), custom_call_target="tpu_custom_call" | custom-call | tf_op jit(solution)/shard_map/dispatch/pallas_call | solution.py:47
  17.9 136.5 %all_to_all.15 = bf16[128,8,5120]{2,1,0:T(8,128)(2,1)} all-to-all(bf16[128,8,5120]{2,1,0:T(8,128)(2,1)S(1)} %bitcast.15), channel_id=1, replica_groups=mesh['group'=8,'inner'=16] {'group','inner'}, dimensions={0} | all-to-all | bytes 20971520 | tf_op jit(solution)/shard_map/all_to_all | solution.py:619
  154.4 29.3 %expert.1 = bf16[1024,2688]{1,0:T(8,128)(2,1)} custom-call(bf16[1024,5120]{1,0:T(8,128)(2,1)} %bitcast.19, bf16[2048,768]{1,0:T(8,128)(2,1)} %bitcast.22, bf16[2048,768]{1,0:T(8,128)(2,1)} %bitcast.23, bf16[768,2048]{1,0:T(8,128)(2,1)} %bitcast.24), custom_call_target="tpu_custom_call" | custom-call | tf_op jit(solution)/shard_map/expert/pallas_call | solution.py:47
  183.7 0.0 copy-start.1
  183.7 0.0 copy-start.2
  183.7 0.0 copy-start.3
  183.7 6.2 %all-to-all-start.1 = ((bf16[128,8,2688]{2,1,0:T(8,128)(2,1)}), bf16[128,8,2688]{2,1,0:T(8,128)(2,1)}, u32[]{:S(2)}, u32[]{:S(2)}) async-start(bf16[128,8,2688]{2,1,0:T(8,128)(2,1)} %bitcast.20), calls=%async_computation.1 | async-start | bytes 11010048 | tf_op jit(solution)/shard_map/all_to_all | solution.py:619
  189.9 2.1 plan.1
  191.9 0.0 copy-start
  192.0 1.4 copy-done
  193.3 9.7 %probs.1 = (bf16[2,2,2560,256]{3,2,1,0:T(8,128)(2,1)}, f32[2048,256]{1,0:T(8,128)}) custom-call(bf16[2048,256]{1,0:T(8,128)(2,1)} %q_ref.2, bf16[2048,256]{1,0:T(8,128)(2,1)} %k_ref.3, bf16[2048,256]{1,0:T(8,128)(2,1)} %v_ref.3), custom_call_target="tpu_custom_call" | custom-call | tf_op jit(solution)/shard_map/probs/pallas_call | solution.py:47
  203.0 52.5 %all-to-all-done.1 = bf16[128,8,2688]{2,1,0:T(8,128)(2,1)} async-done(((bf16[128,8,2688]{2,1,0:T(8,128)(2,1)}), bf16[128,8,2688]{2,1,0:T(8,128)(2,1)}, u32[]{:S(2)}, u32[]{:S(2)}) %all-to-all-start.1) | async-done | bytes 5505056 | tf_op jit(solution)/shard_map/all_to_all | solution.py:619
  255.5 0.0 all-gather.3.cloned.1.call-done
  255.5 0.0 copy-done.1
  255.5 0.0 copy-done.2
  255.5 0.0 copy-done.3
  255.5 14.0 %combine.1 = (bf16[128,2048]{1,0:T(8,128)(2,1)}, bf16[16,2,128,128]{3,2,1,0:T(8,128)(2,1)}) custom-call(bf16[256,1024]{1,0:T(8,128)(2,1)S(1)} %get-tuple-element.40.first_ref, bf16[1024,1024]{1,0:T(8,128)(2,1)} %copy-done, bf16[128,2048]{1,0:T(8,128)(2,1)S(1)} %copy-done.1, bf16[128,2048]{1,0:T(8,128)(2,1)S(1)} %copy-done.2, f32[1,2048]{1,0:T(1,128)S(1)} %bitcast.18, ...), custom_call_target="tpu_custom_call" | custom-call | tf_op jit(solution)/shard_map/combine/pallas_call | solution.py:47
  269.5 3.8 %all-to-all-start.2 = ((bf16[16,256,128]{2,1,0:T(8,128)(2,1)}), bf16[16,256,128]{2,1,0:T(8,128)(2,1)S(1)}, u32[]{:S(2)}, u32[]{:S(2)}) async-start(bf16[16,256,128]{2,1,0:T(8,128)(2,1)} %bitcast.12), calls=%async_computation.2 | async-start | bytes 2097152 | tf_op jit(solution)/shard_map/all_to_all | solution.py:669
  273.3 2.2 scores.1
  275.5 16.0 %all-to-all-done.2 = bf16[16,256,128]{2,1,0:T(8,128)(2,1)S(1)} async-done(((bf16[16,256,128]{2,1,0:T(8,128)(2,1)}), bf16[16,256,128]{2,1,0:T(8,128)(2,1)S(1)}, u32[]{:S(2)}, u32[]{:S(2)}) %all-to-all-start.2) | async-done | bytes 1048608 | tf_op jit(solution)/shard_map/all_to_all | solution.py:669
  291.5 9.1 %attention.1 = (bf16[2048,256]{1,0:T(8,128)(2,1)}, bf16[2048,256]{1,0:T(8,128)(2,1)}, bf16[2048,256]{1,0:T(8,128)(2,1)}) custom-call(bf16[2,2,2560,256]{3,2,1,0:T(8,128)(2,1)} %get-tuple-element.49.probs_ref, f32[2048,256]{1,0:T(8,128)} %get-tuple-element.50.mixed_ref, bf16[16,2,128,128]{3,2,1,0:T(8,128)(2,1)S(1)} %bitcast.16, bf16[2048,256]{1,0:T(8,128)(2,1)} %q_ref.2, ...), custom_call_target="tpu_custom_call" | custom-call | tf_op jit(solution)/shard_map/attention/pallas_call | solution.py:47
Async XLA Ops:
  7.2 248.3 %all-gather.3.cloned.1.call-start = ((), (), s32[]{:S(2)}) async-start(), calls=%async_computation.3 | async-start | bytes 16908288 | tf_op jit(solution)/shard_map/all_gather | solution.py:654
  183.7 71.9 %copy-start.1 = (bf16[128,2048]{1,0:T(8,128)(2,1)S(1)}, bf16[128,2048]{1,0:T(8,128)(2,1)}, u32[]{:S(2)}) copy-start(bf16[128,2048]{1,0:T(8,128)(2,1)} %grad_ref.2) | copy-start | bytes 1572868
  183.7 71.8 %copy-start.2 = (bf16[128,2048]{1,0:T(8,128)(2,1)S(1)}, bf16[128,2048]{1,0:T(8,128)(2,1)}, u32[]{:S(2)}) copy-start(bf16[128,2048]{1,0:T(8,128)(2,1)} %hid_ref.2) | copy-start | bytes 1572868
  183.7 71.8 %copy-start.3 = (f32[2048]{0:T(1024)S(1)}, f32[2048]{0:T(1024)}, u32[]{:S(2)}) copy-start(f32[2048]{0:T(1024)} %param.14) | copy-start | bytes 24580
  183.7 71.8 %all-to-all-start.1 = ((bf16[128,8,2688]{2,1,0:T(8,128)(2,1)}), bf16[128,8,2688]{2,1,0:T(8,128)(2,1)}, u32[]{:S(2)}, u32[]{:S(2)}) async-start(bf16[128,8,2688]{2,1,0:T(8,128)(2,1)} %bitcast.20), calls=%async_computation.1 | async-start | bytes 11010048 | tf_op jit(solution)/shard_map/all_to_all | solution.py:619
  191.9 1.4 copy-start
  269.5 22.0 %all-to-all-start.2 = ((bf16[16,256,128]{2,1,0:T(8,128)(2,1)}), bf16[16,256,128]{2,1,0:T(8,128)(2,1)S(1)}, u32[]{:S(2)}, u32[]{:S(2)}) async-start(bf16[16,256,128]{2,1,0:T(8,128)(2,1)} %bitcast.12), calls=%async_computation.2 | async-start | bytes 2097152 | tf_op jit(solution)/shard_map/all_to_all | solution.py:669
Sparse Core Ops, SparseCore 0:
  12.4 177.4 all-gather.2

commit v5 on v4

--- a/solution.py
+++ b/solution.py
@@ -73,21 +73,21 @@
     )
 
 
-def own_rows_kernel(place_ref, proj_hbm, own_hbm, sem):
-    piece = own_hbm.shape[0]
-    begin = pl.multiple_of(place_ref[0] * piece, piece)
-    own = pltpu.make_async_copy(proj_hbm.at[pl.ds(begin, piece)], own_hbm, sem)
-    own.start()
-    own.wait()
+def own_rows_kernel(place_ref, proj_ref, own_ref):
+    own_ref[...] = proj_ref[...]
 
 
 def own_rows(place, proj, pieces):
+    block = (proj.shape[0] // pieces, proj.shape[1])
     return kernel_call(
         own_rows_kernel,
-        out_shape=jax.ShapeDtypeStruct((proj.shape[0] // pieces, proj.shape[1]), BF),
-        in_specs=[pl.BlockSpec(memory_space=pltpu.SMEM), RAW],
-        out_specs=RAW,
-        scratch_shapes=[pltpu.SemaphoreType.DMA(())],
+        out_shape=jax.ShapeDtypeStruct(block, BF),
+        grid_spec=pltpu.PrefetchScalarGridSpec(
+            num_scalar_prefetch=1,
+            grid=(1,),
+            in_specs=[pl.BlockSpec(block, lambda i, place: (place[0], 0))],
+            out_specs=pl.BlockSpec(block, lambda i, place: (0, 0)),
+        ),
         vmem=16,
         free=(0,),
         name="own_rows",
@@ -165,20 +165,7 @@
 
 
 def expert_kernel(
-    rows_hbm,
-    gate_hbm,
-    up_hbm,
-    down_hbm,
-    out_hbm,
-    rows_ref,
-    gate_ref,
-    up_ref,
-    down_ref,
-    late_ref,
-    act_ref,
-    out_ref,
-    in_sems,
-    out_sems,
+    rows_ref, gate_ref, up_ref, down_ref, out_hbm, late_ref, act_ref, out_ref, out_sems
 ):
     width, hidden = gate_ref.shape
     rows = rows_ref.shape[0]
@@ -187,31 +174,9 @@
     quarter = width // PARTS
     chunk = 256
 
-    def fetch(source, target, n):
-        copy = pltpu.make_async_copy(source, target, in_sems.at[n])
-        copy.start()
-        return copy
-
-    def columns(lo, first, last, n):
-        at = (slice(lo, lo + group), slice(first, last))
-        return fetch(rows_hbm.at[at], rows_ref.at[at], n)
-
-    norm_0 = columns(0, width, 2 * width, 0)
-    gate_in = fetch(gate_hbm, gate_ref, 1)
-    up_in = fetch(up_hbm, up_ref, 2)
-    grad_0 = columns(0, 0, width, 3)
-    down_in = fetch(down_hbm, down_ref, 4)
-    all_1 = columns(group, 0, 2 * width, 5)
-    late_0 = columns(0, 2 * width, 2 * width + 2 * quarter, 6)
-    late_1 = columns(group, 2 * width, 2 * width + 2 * quarter, 7)
-
-    def backward(norm, grad, before_up=(), before_grad=(), acts=None):
+    def backward(norm, grad, acts):
         gate_pre = dot_nn(norm(), gate_ref[...])
-        for copy in before_up:
-            copy.wait()
         up_pre = dot_nn(norm(), up_ref[...])
-        for copy in before_grad:
-            copy.wait()
         score = None
         for col in range(0, hidden, chunk):
             cols = slice(col, col + chunk)
@@ -242,26 +207,15 @@
     main_scores = []
     for index in range(2):
         at = slice(index * group, (index + 1) * group)
-        if index == 0:
-            norm_0.wait()
-            gate_in.wait()
-            waits = ((up_in,), (grad_0, down_in))
-        else:
-            all_1.wait()
-            waits = ((), ())
         acts = act_ref.at[at]
         main_scores.append(
-            backward(
-                lambda: rows_ref[at, width : 2 * width], lambda: rows_ref[at, :width], *waits, acts
-            )
+            backward(lambda: rows_ref[at, width : 2 * width], lambda: rows_ref[at, :width], acts)
         )
         for col in range(0, width, quarter):
             cols = slice(col, col + quarter)
             out_ref[at, cols] = pair(acts, cols)
         send(index * group, group, 0, width)
 
-    late_0.wait()
-    late_1.wait()
     half = group // 2
     few = half // SLOTS * EXTRA
     order = iota((half, half), 0)
@@ -275,7 +229,7 @@
             )
     acts = act_ref.at[rows:]
     late_score = backward(
-        lambda: late_ref[:, width : 2 * width], lambda: late_ref[:, :width], acts=acts
+        lambda: late_ref[:, width : 2 * width], lambda: late_ref[:, :width], acts
     )
     ends = [pair(acts, slice(col, col + quarter)) for col in range(0, width, quarter)]
     order = iota((half, half), 1)
@@ -308,20 +262,16 @@
     return kernel_call(
         expert_kernel,
         out_shape=jax.ShapeDtypeStruct(out_shape, BF),
-        in_specs=[RAW] * 4,
+        in_specs=[HELD] * 4,
         out_specs=RAW,
         scratch_shapes=[
-            pltpu.VMEM(arrived.shape, BF),
-            pltpu.VMEM(gate_mat.shape, BF),
-            pltpu.VMEM(up_mat.shape, BF),
-            pltpu.VMEM(down_mat.shape, BF),
             pltpu.VMEM((late, 2 * width), BF),
             pltpu.VMEM((rows + late, 2 * hidden), BF),
             pltpu.VMEM(out_shape, BF),
-            pltpu.SemaphoreType.DMA((8,)),
             pltpu.SemaphoreType.DMA((3,)),
         ],
-        vmem=48,
+        vmem=24,
+        free=(0, 1, 2, 3),
         name="expert",
     )(arrived, gate_mat, up_mat, down_mat)
 

time: 308 us -> 301 us (0.977)
  Pallas kernels: 76.9 us -> 68.4 us
    pallas_call x8, Pallas kernels: 76.9 us -> 68.4 us  [kernel_call(): call(*[arg if n in free else pin(arg) for n, arg in enumerate(args)])]
  transfers between devices with their start and end apart: 3 -> 3, of which waited for: 2 -> 2; matrix products, arithmetic and copies ran while one was open for 0% -> 0% of each run, Pallas kernels for 16% -> 15%
where the time goes in v5:
time: 301 us; the launch traced here: 300 us
  blocking collectives  137 us (46%)
  waiting for transfers between devices  69.7 us (23%)
  Pallas kernels  68.4 us (23%)
  between operations  14.1 us (5%)
  starting transfers between devices  10 us (3%)
    all_to_all x1, blocking collectives, exchange(): lax.all_to_all(rows.reshape(experts, SLOTS, total), ('group', 'inner'), s...  137 us
    pallas_call x8, Pallas kernels, kernel_call(): call(*[arg if n in free else pin(arg) for n, arg in enumerate(args)])  68.4 us
    all_to_all x1, waiting for transfers between devices, exchange(): lax.all_to_all(rows.reshape(experts, SLOTS, total), ('group', 'inner'), s...  54.2 us
    all_to_all x1, waiting for transfers between devices, local(): lax.all_to_all(grad_attn.reshape(owners, heads * tokens, HD), 'inner', sp...  15.5 us
  transfers between devices with their start and end apart: 3, of which 2 were waited for; matrix products, arithmetic and copies ran while one was open for 0% of the time, Pallas kernels for 15%

profile of v5, /device:TPU:0, one launch (start us, length us, event | category | flops | bytes accessed | tf_op | source)
XLA Modules:
  0.0 300.4 jit_solution(17326958011717222970)
XLA Ops:
  7.2 0.0 all-gather.3.cloned.1.call-start
  7.2 1.6 own_rows.1
  8.8 0.0 all-gather.3.cloned.1.call-update
  8.8 5.5 %dispatch.1 = bf16[1024,5120]{1,0:T(8,128)(2,1)S(1)} custom-call(s32[8,128]{1,0:T(8,128)} %bitcast.25, bf16[128,2048]{1,0:T(8,128)(2,1)} %grad_ref.2, bf16[128,2048]{1,0:T(8,128)(2,1)} %hid_ref.2, f32[1,2048]{1,0:T(1,128)} %bitcast.21), custom_call_target="tpu_custom_call" | custom-call | tf_op jit(solution)/shard_map/dispatch/pallas_call | solution.py:47
  14.4 0.0 copy-start
  14.4 0.0 copy-start.1
  14.4 0.0 copy-start.2
  14.4 136.8 %all_to_all.15 = bf16[128,8,5120]{2,1,0:T(8,128)(2,1)S(1)} all-to-all(bf16[128,8,5120]{2,1,0:T(8,128)(2,1)S(1)} %bitcast.16), channel_id=1, replica_groups=mesh['group'=8,'inner'=16] {'group','inner'}, dimensions={0} | all-to-all | bytes 20971520 | tf_op jit(solution)/shard_map/all_to_all | solution.py:569
  151.2 0.0 copy-done
  151.2 0.0 copy-done.1
  151.2 0.0 copy-done.2
  151.2 24.3 %expert.1 = bf16[1024,2688]{1,0:T(8,128)(2,1)} custom-call(bf16[1024,5120]{1,0:T(8,128)(2,1)S(1)} %bitcast.15, bf16[2048,768]{1,0:T(8,128)(2,1)S(1)} %bitcast.18, bf16[2048,768]{1,0:T(8,128)(2,1)S(1)} %bitcast.19, bf16[768,2048]{1,0:T(8,128)(2,1)S(1)} %bitcast.20), custom_call_target="tpu_custom_call" | custom-call | tf_op jit(solution)/shard_map/expert/pallas_call | solution.py:47
  175.5 0.0 copy-start.4
  175.5 0.0 copy-start.5
  175.5 0.0 copy-start.6
  175.5 6.0 %all-to-all-start.1 = ((bf16[128,8,2688]{2,1,0:T(8,128)(2,1)}), bf16[128,8,2688]{2,1,0:T(8,128)(2,1)}, u32[]{:S(2)}, u32[]{:S(2)}) async-start(bf16[128,8,2688]{2,1,0:T(8,128)(2,1)} %bitcast.23), calls=%async_computation.1 | async-start | bytes 11010048 | tf_op jit(solution)/shard_map/all_to_all | solution.py:569
  181.5 2.1 plan.1
  183.6 0.0 copy-start.3
  183.6 1.3 copy-done.3
  184.9 9.7 %probs.1 = (bf16[2,2,2560,256]{3,2,1,0:T(8,128)(2,1)}, f32[2048,256]{1,0:T(8,128)}) custom-call(bf16[2048,256]{1,0:T(8,128)(2,1)} %q_ref.2, bf16[2048,256]{1,0:T(8,128)(2,1)} %k_ref.3, bf16[2048,256]{1,0:T(8,128)(2,1)} %v_ref.3), custom_call_target="tpu_custom_call" | custom-call | tf_op jit(solution)/shard_map/probs/pallas_call | solution.py:47
  194.6 54.2 %all-to-all-done.1 = bf16[128,8,2688]{2,1,0:T(8,128)(2,1)} async-done(((bf16[128,8,2688]{2,1,0:T(8,128)(2,1)}), bf16[128,8,2688]{2,1,0:T(8,128)(2,1)}, u32[]{:S(2)}, u32[]{:S(2)}) %all-to-all-start.1) | async-done | bytes 5505056 | tf_op jit(solution)/shard_map/all_to_all | solution.py:569
  248.8 0.0 all-gather.3.cloned.1.call-done
  248.8 0.0 copy-done.4
  248.8 0.0 copy-done.5
  248.8 0.0 copy-done.6
  248.8 14.0 %combine.1 = (bf16[128,2048]{1,0:T(8,128)(2,1)}, bf16[16,2,128,128]{3,2,1,0:T(8,128)(2,1)}) custom-call(bf16[256,1024]{1,0:T(8,128)(2,1)S(1)} %get-tuple-element.40.first_ref, bf16[1024,1024]{1,0:T(8,128)(2,1)} %copy-done.3, bf16[128,2048]{1,0:T(8,128)(2,1)S(1)} %copy-done.4, bf16[128,2048]{1,0:T(8,128)(2,1)S(1)} %copy-done.5, f32[1,2048]{1,0:T(1,128)S(1)} %bitcast.22, ...), custom_call_target="tpu_custom_call" | custom-call | tf_op jit(solution)/shard_map/combine/pallas_call | solution.py:47
  262.7 4.0 %all-to-all-start.2 = ((bf16[16,256,128]{2,1,0:T(8,128)(2,1)}), bf16[16,256,128]{2,1,0:T(8,128)(2,1)S(1)}, u32[]{:S(2)}, u32[]{:S(2)}) async-start(bf16[16,256,128]{2,1,0:T(8,128)(2,1)} %bitcast.12), calls=%async_computation.2 | async-start | bytes 2097152 | tf_op jit(solution)/shard_map/all_to_all | solution.py:619
  266.7 2.2 scores.1
  269.0 15.5 %all-to-all-done.2 = bf16[16,256,128]{2,1,0:T(8,128)(2,1)S(1)} async-done(((bf16[16,256,128]{2,1,0:T(8,128)(2,1)}), bf16[16,256,128]{2,1,0:T(8,128)(2,1)S(1)}, u32[]{:S(2)}, u32[]{:S(2)}) %all-to-all-start.2) | async-done | bytes 1048608 | tf_op jit(solution)/shard_map/all_to_all | solution.py:619
  284.5 9.1 %attention.1 = (bf16[2048,256]{1,0:T(8,128)(2,1)}, bf16[2048,256]{1,0:T(8,128)(2,1)}, bf16[2048,256]{1,0:T(8,128)(2,1)}) custom-call(bf16[2,2,2560,256]{3,2,1,0:T(8,128)(2,1)} %get-tuple-element.49.probs_ref, f32[2048,256]{1,0:T(8,128)} %get-tuple-element.50.mixed_ref, bf16[16,2,128,128]{3,2,1,0:T(8,128)(2,1)S(1)} %bitcast.17, bf16[2048,256]{1,0:T(8,128)(2,1)} %q_ref.2, ...), custom_call_target="tpu_custom_call" | custom-call | tf_op jit(solution)/shard_map/attention/pallas_call | solution.py:47
Async XLA Ops:
  7.2 241.6 %all-gather.3.cloned.1.call-start = ((), (), s32[]{:S(2)}) async-start(), calls=%async_computation.3 | async-start | bytes 16908288 | tf_op jit(solution)/shard_map/all_gather | solution.py:604
  14.4 136.8 %copy-start = (bf16[1,2048,768]{2,1,0:T(8,128)(2,1)S(1)}, bf16[1,2048,768]{2,1,0:T(8,128)(2,1)}, u32[]{:S(2)}) copy-start(bf16[1,2048,768]{2,1,0:T(8,128)(2,1)} %param.17) | copy-start | bytes 9437188
  14.4 136.8 %copy-start.1 = (bf16[1,2048,768]{2,1,0:T(8,128)(2,1)S(1)}, bf16[1,2048,768]{2,1,0:T(8,128)(2,1)}, u32[]{:S(2)}) copy-start(bf16[1,2048,768]{2,1,0:T(8,128)(2,1)} %param.18) | copy-start | bytes 9437188
  14.4 136.8 %copy-start.2 = (bf16[1,768,2048]{2,1,0:T(8,128)(2,1)S(1)}, bf16[1,768,2048]{2,1,0:T(8,128)(2,1)}, u32[]{:S(2)}) copy-start(bf16[1,768,2048]{2,1,0:T(8,128)(2,1)} %param.19) | copy-start | bytes 9437188
  175.5 73.3 %copy-start.4 = (bf16[128,2048]{1,0:T(8,128)(2,1)S(1)}, bf16[128,2048]{1,0:T(8,128)(2,1)}, u32[]{:S(2)}) copy-start(bf16[128,2048]{1,0:T(8,128)(2,1)} %grad_ref.2) | copy-start | bytes 1572868
  175.5 73.3 %copy-start.5 = (bf16[128,2048]{1,0:T(8,128)(2,1)S(1)}, bf16[128,2048]{1,0:T(8,128)(2,1)}, u32[]{:S(2)}) copy-start(bf16[128,2048]{1,0:T(8,128)(2,1)} %hid_ref.2) | copy-start | bytes 1572868
  175.5 73.3 %copy-start.6 = (f32[2048]{0:T(1024)S(1)}, f32[2048]{0:T(1024)}, u32[]{:S(2)}) copy-start(f32[2048]{0:T(1024)} %param.14) | copy-start | bytes 24580
  175.5 73.2 %all-to-all-start.1 = ((bf16[128,8,2688]{2,1,0:T(8,128)(2,1)}), bf16[128,8,2688]{2,1,0:T(8,128)(2,1)}, u32[]{:S(2)}, u32[]{:S(2)}) async-start(bf16[128,8,2688]{2,1,0:T(8,128)(2,1)} %bitcast.23), calls=%async_computation.1 | async-start | bytes 11010048 | tf_op jit(solution)/shard_map/all_to_all | solution.py:569
  183.6 1.3 copy-start.3
  262.7 21.7 %all-to-all-start.2 = ((bf16[16,256,128]{2,1,0:T(8,128)(2,1)}), bf16[16,256,128]{2,1,0:T(8,128)(2,1)S(1)}, u32[]{:S(2)}, u32[]{:S(2)}) async-start(bf16[16,256,128]{2,1,0:T(8,128)(2,1)} %bitcast.12), calls=%async_computation.2 | async-start | bytes 2097152 | tf_op jit(solution)/shard_map/all_to_all | solution.py:619
Sparse Core Ops, SparseCore 0:
  11.7 177.3 all-gather.2

commit v6 on v5

--- a/solution.py
+++ b/solution.py
@@ -12,7 +12,7 @@
 SLOTS = 8
 EXTRA = 2
 PARTS = 4
-LANES = 128
+PLACES = 16
 BF = jnp.bfloat16
 F32 = jnp.float32
 
@@ -66,10 +66,10 @@
     return jnp.where(member > 0.5, slot, -1.0)
 
 
-def per_row(by_expert):
+def per_row(by_expert, count=SLOTS):
     experts, width = by_expert.shape
-    return jnp.broadcast_to(by_expert[:, None, :], (experts, SLOTS, width)).reshape(
-        experts * SLOTS, width
+    return jnp.broadcast_to(by_expert[:, None, :], (experts, count, width)).reshape(
+        experts * count, width
     )
 
 
@@ -165,7 +165,7 @@
 
 
 def expert_kernel(
-    rows_ref, gate_ref, up_ref, down_ref, out_hbm, late_ref, act_ref, out_ref, out_sems
+    rows_ref, gate_ref, up_ref, down_ref, out_hbm, score_ref, late_ref, act_ref, out_ref, out_sems
 ):
     width, hidden = gate_ref.shape
     rows = rows_ref.shape[0]
@@ -236,20 +236,23 @@
     scatter = jnp.where(
         iota((half, half), 0) == (order % few) * PARTS + order // few, 1.0, 0.0
     ).astype(BF)
-    spread = jnp.where((iota((half, few), 0) >> 2) == iota((half, few), 1), 1.0, 0.0).astype(BF)
-    lane = iota((half, LANES), 1)
     for block in range(rows // half):
         at = slice(block * half, (block + 1) * half)
         own = slice(block * few, (block + 1) * few)
         stacked = jnp.concatenate([end[own] for end in ends], axis=0)
         out_ref[at, width : width + quarter] = dot_nn(scatter, stacked).astype(BF)
-        spread_score = dot_nn(spread, jnp.broadcast_to(late_score[own], (few, LANES)).astype(BF))
-        start = (block % 2) * half
-        main_score = main_scores[block // 2][start : start + half]
-        out_ref[at, width + quarter :] = jnp.where(
-            lane == 0, main_score, jnp.where(lane == 1, spread_score, 0.0)
-        ).astype(BF)
-    send(0, rows, width, width + quarter + LANES)
+    send(0, rows, width, width + quarter)
+
+    def by_source(score, count, base):
+        height = score.shape[0]
+        sources = score_ref.shape[1]
+        place = base + (iota((height, PLACES), 0) & (count - 1))
+        values = jnp.where(place == iota((height, PLACES), 1), score, 0.0).astype(BF)
+        source = iota((height, sources), 0) // count == iota((height, sources), 1)
+        return dot_tn(values, jnp.where(source, 1.0, 0.0).astype(BF))
+
+    scores_main = by_source(jnp.concatenate(main_scores, axis=0), SLOTS, 0)
+    score_ref[...] = (scores_main + by_source(late_score, EXTRA, SLOTS)).astype(BF)
     for copy in sent:
         copy.wait()
 
@@ -258,12 +261,15 @@
     rows = arrived.shape[0]
     width, hidden = gate_mat.shape
     late = rows // SLOTS * EXTRA
-    out_shape = (rows, width + width // PARTS + LANES)
+    out_shape = (rows, width + width // PARTS)
     return kernel_call(
         expert_kernel,
-        out_shape=jax.ShapeDtypeStruct(out_shape, BF),
+        out_shape=(
+            jax.ShapeDtypeStruct(out_shape, BF),
+            jax.ShapeDtypeStruct((PLACES, rows // SLOTS), BF),
+        ),
         in_specs=[HELD] * 4,
-        out_specs=RAW,
+        out_specs=(RAW, pl.BlockSpec((PLACES, rows // SLOTS), lambda: (0, 0))),
         scratch_shapes=[
             pltpu.VMEM((late, 2 * width), BF),
             pltpu.VMEM((rows + late, 2 * hidden), BF),
@@ -321,7 +327,7 @@
 
 def combine_kernel(
     first_ref,
-    late_ref,
+    late_hbm,
     grad_ref,
     hid_ref,
     gain_ref,
@@ -331,6 +337,7 @@
     attn_ref,
     back_ref,
     proj_ref,
+    late_ref,
     sems,
 ):
     tokens, width = grad_ref.shape
@@ -344,6 +351,7 @@
         copy.start()
         return copy
 
+    late_in = fetch(late_hbm, late_ref, PARTS + 9)
     backs = []
     for n, part in enumerate((PARTS,) + tuple(range(PARTS))):
         at = (slice(None), slice(part * quarter, (part + 1) * quarter))
@@ -357,6 +365,7 @@
 
     hid = hid_ref[...].astype(F32)
     inv_rms = lax.rsqrt(jnp.mean(hid * hid, axis=1, keepdims=True) + 1e-06)
+    late_in.wait()
     backs[0].wait()
     late = dot_nn(late_ref[...], back_ref[:, width:])
     total = jnp.zeros((tokens, 1), F32)
@@ -401,12 +410,13 @@
             jax.ShapeDtypeStruct(grad_out.shape, BF),
             jax.ShapeDtypeStruct((owners, heads, tokens, HD), BF),
         ),
-        in_specs=[HELD] * 5 + [RAW] * 2,
+        in_specs=[HELD, RAW] + [HELD] * 3 + [RAW] * 2,
         out_specs=(HELD, HELD),
         scratch_shapes=[
             pltpu.VMEM((back.shape[0], width + width // PARTS), BF),
             pltpu.VMEM(proj.shape, BF),
-            pltpu.SemaphoreType.DMA((PARTS + 9,)),
+            pltpu.VMEM(late.shape, BF),
+            pltpu.SemaphoreType.DMA((PARTS + 10,)),
         ],
         vmem=50,
         space=None,
@@ -415,17 +425,17 @@
     )(first, late, grad_out, hidden_in, gain, back, proj)
 
 
-def score_kernel(ids_ref, score_ref, gate_ref):
+def score_kernel(me_ref, ids_ref, score_ref, gate_ref):
     ids = ids_ref[...]
     top, tokens = ids.shape
-    rows = score_ref.shape[0]
-    experts = rows // SLOTS
-    score = score_ref[...].astype(F32)
-    first, late, place = placed(ids, rows)
-    got = jnp.where(first, score[:, 0:1], 0.0) + jnp.where(
-        late & ((place & (PARTS - 1)) == 0), score[:, 1:2], 0.0
-    )
-    by_expert = jnp.sum(got.reshape(experts, SLOTS, tokens), axis=1)
+    rows, devices = score_ref.shape
+    experts = rows // PLACES
+    mine = iota((rows, devices), 1) == me_ref[0]
+    score = jnp.sum(jnp.where(mine, score_ref[...].astype(F32), 0.0), axis=1, keepdims=True)
+    slot = per_row(routing(ids, experts), PLACES)
+    place = iota(slot.shape, 0) & (PLACES - 1)
+    got = jnp.where(slot == place.astype(F32), score, 0.0)
+    by_expert = jnp.sum(got.reshape(experts, PLACES, tokens), axis=1)
     row = iota((experts, tokens), 0)
     gates = [
         jnp.sum(jnp.where(ids[k : k + 1, :] == row, by_expert, 0.0), axis=0, keepdims=True)
@@ -434,20 +444,21 @@
     gate_ref[...] = jnp.concatenate(gates, axis=0).astype(BF)
 
 
-def scores(ids, back):
-    rows, total = back.shape
+def scores(me, ids, gathered):
     return kernel_call(
         score_kernel,
         out_shape=jax.ShapeDtypeStruct(ids.shape, BF),
         grid=(1,),
         in_specs=[
+            pl.BlockSpec(memory_space=pltpu.SMEM),
             whole(ids.shape),
-            pl.BlockSpec((rows, LANES), lambda i: (0, total // LANES - 1)),
+            whole(gathered.shape),
         ],
         out_specs=whole(ids.shape),
         vmem=16,
+        free=(0,),
         name="scores",
-    )(ids, back)
+    )(me, ids, gathered)
 
 
 BLOCK = 256
@@ -604,7 +615,8 @@
     proj = lax.all_gather(own_proj, ("group", "inner"), axis=0, tiled=False)
     outgoing = dispatch(ids, grad_now, hidden_now, gain, experts)
     arrived = exchange(outgoing, experts)
-    answers = expert_backward(arrived, gate_proj[0], up_proj[0], down_proj[0])
+    answers, own_scores = expert_backward(arrived, gate_proj[0], up_proj[0], down_proj[0])
+    all_scores = lax.all_gather(own_scores, ("group", "inner"), axis=0, tiled=True)
     answers, ids_late, query = lax.optimization_barrier((answers, ids, query_rows))
     back = exchange(answers, experts)
     probs, mixed = attention_probs(query, key_rows, value_rows)
@@ -614,8 +626,8 @@
         first, late, grad_out, hidden_in, gain, back, proj.reshape(groups, owners, piece, width)
     )
     heads = grad_attn.shape[1]
-    grad_attn, back = lax.optimization_barrier((grad_attn, back))
-    grad_gate = scores(ids, back).T
+    grad_attn, all_scores = lax.optimization_barrier((grad_attn, all_scores))
+    grad_gate = scores(lax.axis_index(("group", "inner")).reshape(1), ids, all_scores).T
     grad_attn = lax.all_to_all(
         grad_attn.reshape(owners, heads * tokens, HD),
         "inner",

time: 301 us -> 342 us (1.14)
  blocking collectives: 137 us -> 231 us
  waiting for transfers between devices: 69.7 us -> 16.3 us
    all_gather x0 -> x1, blocking collectives: none -> 94.3 us  [local(): lax.all_gather(own_scores, ('group', 'inner'), axis=0, tiled=True)]
    all_to_all x1, waiting for transfers between devices: 54.2 us -> 0.01 us  [exchange(): lax.all_to_all(rows.reshape(experts, SLOTS, total), ('group', 'inner'), s...]
  transfers between devices with their start and end apart: 3 -> 3, of which waited for: 2 -> 1; matrix products, arithmetic and copies ran while one was open for 0% -> 0% of each run, Pallas kernels for 15% -> 13%
where the time goes in v6:
time: 342 us; the launch traced here: 341 us
  blocking collectives  231 us (68%)
  Pallas kernels  68.3 us (20%)
  waiting for transfers between devices  16.3 us (5%)
  between operations  14.2 us (4%)
  starting transfers between devices  9.84 us (3%)
    all_to_all x1, blocking collectives, exchange(): lax.all_to_all(rows.reshape(experts, SLOTS, total), ('group', 'inner'), s...  137 us
    all_gather x1, blocking collectives, local(): lax.all_gather(own_scores, ('group', 'inner'), axis=0, tiled=True)  94.3 us
    pallas_call x8, Pallas kernels, kernel_call(): call(*[arg if n in free else pin(arg) for n, arg in enumerate(args)])  68.3 us
    all_to_all x1, waiting for transfers between devices, local(): lax.all_to_all(grad_attn.reshape(owners, heads * tokens, HD), 'inner', sp...  16.2 us
  transfers between devices with their start and end apart: 3, of which 1 were waited for; matrix products, arithmetic and copies ran while one was open for 0% of the time, Pallas kernels for 13%

profile of v6, /device:TPU:0, one launch (start us, length us, event | category | flops | bytes accessed | tf_op | source)
XLA Modules:
  0.0 341.1 jit_solution(1134673190900663996)
XLA Ops:
  7.2 0.0 all-gather.3.cloned.1.call-start
  7.2 1.6 own_rows.1
  8.8 0.0 all-gather.3.cloned.1.call-update
  8.8 5.5 %dispatch.1 = bf16[1024,5120]{1,0:T(8,128)(2,1)S(1)} custom-call(s32[8,128]{1,0:T(8,128)} %bitcast.26, bf16[128,2048]{1,0:T(8,128)(2,1)} %grad_ref.2, bf16[128,2048]{1,0:T(8,128)(2,1)} %hid_ref.2, f32[1,2048]{1,0:T(1,128)} %bitcast.22), custom_call_target="tpu_custom_call" | custom-call | tf_op jit(solution)/shard_map/dispatch/pallas_call | solution.py:47
  14.4 0.0 copy-start
  14.4 0.0 copy-start.1
  14.4 0.0 copy-start.2
  14.4 136.8 %all_to_all.15 = bf16[128,8,5120]{2,1,0:T(8,128)(2,1)S(1)} all-to-all(bf16[128,8,5120]{2,1,0:T(8,128)(2,1)S(1)} %bitcast.17), channel_id=1, replica_groups=mesh['group'=8,'inner'=16] {'group','inner'}, dimensions={0} | all-to-all | bytes 20971520 | tf_op jit(solution)/shard_map/all_to_all | solution.py:580
  151.2 0.0 copy-done
  151.2 0.0 copy-done.1
  151.2 0.0 copy-done.2
  151.2 24.7 %expert.1 = (bf16[1024,2560]{1,0:T(8,128)(2,1)}, bf16[16,128]{1,0:T(8,128)(2,1)}) custom-call(bf16[1024,5120]{1,0:T(8,128)(2,1)S(1)} %bitcast.16, bf16[2048,768]{1,0:T(8,128)(2,1)S(1)} %bitcast.19, bf16[2048,768]{1,0:T(8,128)(2,1)S(1)} %bitcast.20, bf16[768,2048]{1,0:T(8,128)(2,1)S(1)} %bitcast.21), custom_call_target="tpu_custom_call" | custom-call | tf_op jit(solution)/shard_map/expert/pallas_call | solution.py:47
  176.0 0.0 copy-start.7
  176.0 0.0 copy-start.4
  176.0 0.0 copy-start.5
  176.0 0.0 copy-start.6
  176.0 5.9 %all-to-all-start.1 = ((bf16[128,8,2560]{2,1,0:T(8,128)(2,1)}), bf16[128,8,2560]{2,1,0:T(8,128)(2,1)}, u32[]{:S(2)}, u32[]{:S(2)}) async-start(bf16[128,8,2560]{2,1,0:T(8,128)(2,1)} %bitcast.25), calls=%async_computation.1 | async-start | bytes 10485760 | tf_op jit(solution)/shard_map/all_to_all | solution.py:580
  182.0 2.1 plan.1
  184.1 0.0 copy-start.3
  184.1 1.3 copy-done.3
  185.4 9.8 %probs.1 = (bf16[2,2,2560,256]{3,2,1,0:T(8,128)(2,1)}, f32[2048,256]{1,0:T(8,128)}) custom-call(bf16[2048,256]{1,0:T(8,128)(2,1)} %q_ref.2, bf16[2048,256]{1,0:T(8,128)(2,1)} %k_ref.3, bf16[2048,256]{1,0:T(8,128)(2,1)} %v_ref.3), custom_call_target="tpu_custom_call" | custom-call | tf_op jit(solution)/shard_map/probs/pallas_call | solution.py:47
  195.1 0.0 copy-done.7
  195.1 94.3 %all_gather.11.score_ref = bf16[2048,128]{1,0:T(8,128)(2,1)} all-gather(bf16[16,128]{1,0:T(8,128)(2,1)S(1)} %copy-done.7), channel_id=1, replica_groups=mesh['group'=8,'inner'=16] {'group','inner'}, dimensions={0}, use_global_device_ids=true | all-gather | bytes 528384 | tf_op jit(solution)/shard_map/all_gather | solution.py:619
  289.4 0.0 all-to-all-done.1
  289.4 0.0 all-gather.3.cloned.1.call-done
  289.5 0.0 copy-done.4
  289.5 0.0 copy-done.5
  289.5 13.2 %combine.1 = (bf16[128,2048]{1,0:T(8,128)(2,1)}, bf16[16,2,128,128]{3,2,1,0:T(8,128)(2,1)}) custom-call(bf16[256,1024]{1,0:T(8,128)(2,1)S(1)} %get-tuple-element.43.first_ref, bf16[1024,1024]{1,0:T(8,128)(2,1)} %copy-done.3, bf16[128,2048]{1,0:T(8,128)(2,1)S(1)} %copy-done.4, bf16[128,2048]{1,0:T(8,128)(2,1)S(1)} %copy-done.5, f32[1,2048]{1,0:T(1,128)S(1)} %bitcast.23, ...), custom_call_target="tpu_custom_call" | custom-call | tf_op jit(solution)/shard_map/combine/pallas_call | solution.py:47
  302.7 3.9 %all-to-all-start.2 = ((bf16[16,256,128]{2,1,0:T(8,128)(2,1)}), bf16[16,256,128]{2,1,0:T(8,128)(2,1)S(1)}, u32[]{:S(2)}, u32[]{:S(2)}) async-start(bf16[16,256,128]{2,1,0:T(8,128)(2,1)} %bitcast.12), calls=%async_computation.2 | async-start | bytes 2097152 | tf_op jit(solution)/shard_map/all_to_all | solution.py:631
  306.6 2.3 scores.1
  308.9 16.2 %all-to-all-done.2 = bf16[16,256,128]{2,1,0:T(8,128)(2,1)S(1)} async-done(((bf16[16,256,128]{2,1,0:T(8,128)(2,1)}), bf16[16,256,128]{2,1,0:T(8,128)(2,1)S(1)}, u32[]{:S(2)}, u32[]{:S(2)}) %all-to-all-start.2) | async-done | bytes 1048608 | tf_op jit(solution)/shard_map/all_to_all | solution.py:631
  325.1 9.1 %attention.1 = (bf16[2048,256]{1,0:T(8,128)(2,1)}, bf16[2048,256]{1,0:T(8,128)(2,1)}, bf16[2048,256]{1,0:T(8,128)(2,1)}) custom-call(bf16[2,2,2560,256]{3,2,1,0:T(8,128)(2,1)} %get-tuple-element.53.probs_ref, f32[2048,256]{1,0:T(8,128)} %get-tuple-element.54.mixed_ref, bf16[16,2,128,128]{3,2,1,0:T(8,128)(2,1)S(1)} %bitcast.18, bf16[2048,256]{1,0:T(8,128)(2,1)} %q_ref.2, ...), custom_call_target="tpu_custom_call" | custom-call | tf_op jit(solution)/shard_map/attention/pallas_call | solution.py:47
  (1 shorter events, 0.0 us)
Async XLA Ops:
  7.2 282.3 %all-gather.3.cloned.1.call-start = ((), (), s32[]{:S(2)}) async-start(), calls=%async_computation.3 | async-start | bytes 16908288 | tf_op jit(solution)/shard_map/all_gather | solution.py:615
  14.4 136.9 %copy-start = (bf16[1,2048,768]{2,1,0:T(8,128)(2,1)S(1)}, bf16[1,2048,768]{2,1,0:T(8,128)(2,1)}, u32[]{:S(2)}) copy-start(bf16[1,2048,768]{2,1,0:T(8,128)(2,1)} %param.17) | copy-start | bytes 9437188
  14.4 136.8 %copy-start.1 = (bf16[1,2048,768]{2,1,0:T(8,128)(2,1)S(1)}, bf16[1,2048,768]{2,1,0:T(8,128)(2,1)}, u32[]{:S(2)}) copy-start(bf16[1,2048,768]{2,1,0:T(8,128)(2,1)} %param.18) | copy-start | bytes 9437188
  14.4 136.8 %copy-start.2 = (bf16[1,768,2048]{2,1,0:T(8,128)(2,1)S(1)}, bf16[1,768,2048]{2,1,0:T(8,128)(2,1)}, u32[]{:S(2)}) copy-start(bf16[1,768,2048]{2,1,0:T(8,128)(2,1)} %param.19) | copy-start | bytes 9437188
  176.0 19.2 %copy-start.7 = (bf16[16,128]{1,0:T(8,128)(2,1)S(1)}, bf16[16,128]{1,0:T(8,128)(2,1)}, u32[]{:S(2)}) copy-start(bf16[16,128]{1,0:T(8,128)(2,1)} %get-tuple-element.49) | copy-start | bytes 12292
  176.0 113.5 %copy-start.4 = (bf16[128,2048]{1,0:T(8,128)(2,1)S(1)}, bf16[128,2048]{1,0:T(8,128)(2,1)}, u32[]{:S(2)}) copy-start(bf16[128,2048]{1,0:T(8,128)(2,1)} %grad_ref.2) | copy-start | bytes 1572868
  176.0 113.5 %copy-start.5 = (bf16[128,2048]{1,0:T(8,128)(2,1)S(1)}, bf16[128,2048]{1,0:T(8,128)(2,1)}, u32[]{:S(2)}) copy-start(bf16[128,2048]{1,0:T(8,128)(2,1)} %hid_ref.2) | copy-start | bytes 1572868
  176.0 113.5 %copy-start.6 = (f32[2048]{0:T(1024)S(1)}, f32[2048]{0:T(1024)}, u32[]{:S(2)}) copy-start(f32[2048]{0:T(1024)} %param.14) | copy-start | bytes 24580
  176.0 113.4 %all-to-all-start.1 = ((bf16[128,8,2560]{2,1,0:T(8,128)(2,1)}), bf16[128,8,2560]{2,1,0:T(8,128)(2,1)}, u32[]{:S(2)}, u32[]{:S(2)}) async-start(bf16[128,8,2560]{2,1,0:T(8,128)(2,1)} %bitcast.25), calls=%async_computation.1 | async-start | bytes 10485760 | tf_op jit(solution)/shard_map/all_to_all | solution.py:580
  184.1 1.3 copy-start.3
  302.7 22.4 %all-to-all-start.2 = ((bf16[16,256,128]{2,1,0:T(8,128)(2,1)}), bf16[16,256,128]{2,1,0:T(8,128)(2,1)S(1)}, u32[]{:S(2)}, u32[]{:S(2)}) async-start(bf16[16,256,128]{2,1,0:T(8,128)(2,1)} %bitcast.12), calls=%async_computation.2 | async-start | bytes 2097152 | tf_op jit(solution)/shard_map/all_to_all | solution.py:631
Sparse Core Ops, SparseCore 0:
  11.7 175.7 all-gather.2

commit v7 on v5

--- a/solution.py
+++ b/solution.py
@@ -321,7 +321,7 @@
 
 def combine_kernel(
     first_ref,
-    late_ref,
+    late_hbm,
     grad_ref,
     hid_ref,
     gain_ref,
@@ -331,6 +331,7 @@
     attn_ref,
     back_ref,
     proj_ref,
+    late_ref,
     sems,
 ):
     tokens, width = grad_ref.shape
@@ -344,6 +345,7 @@
         copy.start()
         return copy
 
+    late_in = fetch(late_hbm, late_ref, PARTS + 9)
     backs = []
     for n, part in enumerate((PARTS,) + tuple(range(PARTS))):
         at = (slice(None), slice(part * quarter, (part + 1) * quarter))
@@ -357,6 +359,7 @@
 
     hid = hid_ref[...].astype(F32)
     inv_rms = lax.rsqrt(jnp.mean(hid * hid, axis=1, keepdims=True) + 1e-06)
+    late_in.wait()
     backs[0].wait()
     late = dot_nn(late_ref[...], back_ref[:, width:])
     total = jnp.zeros((tokens, 1), F32)
@@ -401,12 +404,13 @@
             jax.ShapeDtypeStruct(grad_out.shape, BF),
             jax.ShapeDtypeStruct((owners, heads, tokens, HD), BF),
         ),
-        in_specs=[HELD] * 5 + [RAW] * 2,
+        in_specs=[HELD, RAW] + [HELD] * 3 + [RAW] * 2,
         out_specs=(HELD, HELD),
         scratch_shapes=[
             pltpu.VMEM((back.shape[0], width + width // PARTS), BF),
             pltpu.VMEM(proj.shape, BF),
-            pltpu.SemaphoreType.DMA((PARTS + 9,)),
+            pltpu.VMEM(late.shape, BF),
+            pltpu.SemaphoreType.DMA((PARTS + 10,)),
         ],
         vmem=50,
         space=None,

time: 301 us -> 300 us (level)
  no operation moved by 1% of the time
where the time goes in v7:
time: 300 us; the launch traced here: 299 us
  blocking collectives  137 us (46%)
  waiting for transfers between devices  69.7 us (23%)
  Pallas kernels  67.5 us (22%)
  between operations  14.1 us (5%)
  starting transfers between devices  10 us (3%)
    all_to_all x1, blocking collectives, exchange(): lax.all_to_all(rows.reshape(experts, SLOTS, total), ('group', 'inner'), s...  137 us
    pallas_call x8, Pallas kernels, kernel_call(): call(*[arg if n in free else pin(arg) for n, arg in enumerate(args)])  67.5 us
    all_to_all x1, waiting for transfers between devices, exchange(): lax.all_to_all(rows.reshape(experts, SLOTS, total), ('group', 'inner'), s...  54.2 us
    all_to_all x1, waiting for transfers between devices, local(): lax.all_to_all(grad_attn.reshape(owners, heads * tokens, HD), 'inner', sp...  15.5 us
  transfers between devices with their start and end apart: 3, of which 2 were waited for; matrix products, arithmetic and copies ran while one was open for 0% of the time, Pallas kernels for 15%

profile of v7, /device:TPU:0, one launch (start us, length us, event | category | flops | bytes accessed | tf_op | source)
XLA Modules:
  0.0 299.5 jit_solution(11892695254343549817)
XLA Ops:
  7.2 0.0 all-gather.3.cloned.1.call-start
  7.2 1.6 own_rows.1
  8.8 0.0 all-gather.3.cloned.1.call-update
  8.8 5.5 %dispatch.1 = bf16[1024,5120]{1,0:T(8,128)(2,1)S(1)} custom-call(s32[8,128]{1,0:T(8,128)} %bitcast.25, bf16[128,2048]{1,0:T(8,128)(2,1)} %grad_ref.2, bf16[128,2048]{1,0:T(8,128)(2,1)} %hid_ref.2, f32[1,2048]{1,0:T(1,128)} %bitcast.21), custom_call_target="tpu_custom_call" | custom-call | tf_op jit(solution)/shard_map/dispatch/pallas_call | solution.py:47
  14.4 0.0 copy-start
  14.4 0.0 copy-start.1
  14.4 0.0 copy-start.2
  14.4 136.8 %all_to_all.15 = bf16[128,8,5120]{2,1,0:T(8,128)(2,1)S(1)} all-to-all(bf16[128,8,5120]{2,1,0:T(8,128)(2,1)S(1)} %bitcast.16), channel_id=1, replica_groups=mesh['group'=8,'inner'=16] {'group','inner'}, dimensions={0} | all-to-all | bytes 20971520 | tf_op jit(solution)/shard_map/all_to_all | solution.py:573
  151.2 0.0 copy-done
  151.2 0.0 copy-done.1
  151.2 0.0 copy-done.2
  151.2 24.3 %expert.1 = bf16[1024,2688]{1,0:T(8,128)(2,1)} custom-call(bf16[1024,5120]{1,0:T(8,128)(2,1)S(1)} %bitcast.15, bf16[2048,768]{1,0:T(8,128)(2,1)S(1)} %bitcast.18, bf16[2048,768]{1,0:T(8,128)(2,1)S(1)} %bitcast.19, bf16[768,2048]{1,0:T(8,128)(2,1)S(1)} %bitcast.20), custom_call_target="tpu_custom_call" | custom-call | tf_op jit(solution)/shard_map/expert/pallas_call | solution.py:47
  175.5 0.0 copy-start.4
  175.5 0.0 copy-start.5
  175.5 0.0 copy-start.6
  175.5 6.0 %all-to-all-start.1 = ((bf16[128,8,2688]{2,1,0:T(8,128)(2,1)}), bf16[128,8,2688]{2,1,0:T(8,128)(2,1)}, u32[]{:S(2)}, u32[]{:S(2)}) async-start(bf16[128,8,2688]{2,1,0:T(8,128)(2,1)} %bitcast.23), calls=%async_computation.1 | async-start | bytes 11010048 | tf_op jit(solution)/shard_map/all_to_all | solution.py:573
  181.5 2.1 plan.1
  183.6 0.0 copy-start.3
  183.6 1.3 copy-done.3
  184.9 9.7 %probs.1 = (bf16[2,2,2560,256]{3,2,1,0:T(8,128)(2,1)}, f32[2048,256]{1,0:T(8,128)}) custom-call(bf16[2048,256]{1,0:T(8,128)(2,1)} %q_ref.2, bf16[2048,256]{1,0:T(8,128)(2,1)} %k_ref.3, bf16[2048,256]{1,0:T(8,128)(2,1)} %v_ref.3), custom_call_target="tpu_custom_call" | custom-call | tf_op jit(solution)/shard_map/probs/pallas_call | solution.py:47
  194.6 54.2 %all-to-all-done.1 = bf16[128,8,2688]{2,1,0:T(8,128)(2,1)} async-done(((bf16[128,8,2688]{2,1,0:T(8,128)(2,1)}), bf16[128,8,2688]{2,1,0:T(8,128)(2,1)}, u32[]{:S(2)}, u32[]{:S(2)}) %all-to-all-start.1) | async-done | bytes 5505056 | tf_op jit(solution)/shard_map/all_to_all | solution.py:573
  248.8 0.0 all-gather.3.cloned.1.call-done
  248.8 0.0 copy-done.4
  248.8 0.0 copy-done.5
  248.8 0.0 copy-done.6
  248.8 13.0 %combine.1 = (bf16[128,2048]{1,0:T(8,128)(2,1)}, bf16[16,2,128,128]{3,2,1,0:T(8,128)(2,1)}) custom-call(bf16[256,1024]{1,0:T(8,128)(2,1)S(1)} %get-tuple-element.40.first_ref, bf16[1024,1024]{1,0:T(8,128)(2,1)} %copy-done.3, bf16[128,2048]{1,0:T(8,128)(2,1)S(1)} %copy-done.4, bf16[128,2048]{1,0:T(8,128)(2,1)S(1)} %copy-done.5, f32[1,2048]{1,0:T(1,128)S(1)} %bitcast.22, ...), custom_call_target="tpu_custom_call" | custom-call | tf_op jit(solution)/shard_map/combine/pallas_call | solution.py:47
  261.8 4.0 %all-to-all-start.2 = ((bf16[16,256,128]{2,1,0:T(8,128)(2,1)}), bf16[16,256,128]{2,1,0:T(8,128)(2,1)S(1)}, u32[]{:S(2)}, u32[]{:S(2)}) async-start(bf16[16,256,128]{2,1,0:T(8,128)(2,1)} %bitcast.12), calls=%async_computation.2 | async-start | bytes 2097152 | tf_op jit(solution)/shard_map/all_to_all | solution.py:623
  265.8 2.2 scores.1
  268.0 15.5 %all-to-all-done.2 = bf16[16,256,128]{2,1,0:T(8,128)(2,1)S(1)} async-done(((bf16[16,256,128]{2,1,0:T(8,128)(2,1)}), bf16[16,256,128]{2,1,0:T(8,128)(2,1)S(1)}, u32[]{:S(2)}, u32[]{:S(2)}) %all-to-all-start.2) | async-done | bytes 1048608 | tf_op jit(solution)/shard_map/all_to_all | solution.py:623
  283.5 9.1 %attention.1 = (bf16[2048,256]{1,0:T(8,128)(2,1)}, bf16[2048,256]{1,0:T(8,128)(2,1)}, bf16[2048,256]{1,0:T(8,128)(2,1)}) custom-call(bf16[2,2,2560,256]{3,2,1,0:T(8,128)(2,1)} %get-tuple-element.49.probs_ref, f32[2048,256]{1,0:T(8,128)} %get-tuple-element.50.mixed_ref, bf16[16,2,128,128]{3,2,1,0:T(8,128)(2,1)S(1)} %bitcast.17, bf16[2048,256]{1,0:T(8,128)(2,1)} %q_ref.2, ...), custom_call_target="tpu_custom_call" | custom-call | tf_op jit(solution)/shard_map/attention/pallas_call | solution.py:47
Async XLA Ops:
  7.2 241.6 %all-gather.3.cloned.1.call-start = ((), (), s32[]{:S(2)}) async-start(), calls=%async_computation.3 | async-start | bytes 16908288 | tf_op jit(solution)/shard_map/all_gather | solution.py:608
  14.4 136.8 %copy-start = (bf16[1,2048,768]{2,1,0:T(8,128)(2,1)S(1)}, bf16[1,2048,768]{2,1,0:T(8,128)(2,1)}, u32[]{:S(2)}) copy-start(bf16[1,2048,768]{2,1,0:T(8,128)(2,1)} %param.17) | copy-start | bytes 9437188
  14.4 136.8 %copy-start.1 = (bf16[1,2048,768]{2,1,0:T(8,128)(2,1)S(1)}, bf16[1,2048,768]{2,1,0:T(8,128)(2,1)}, u32[]{:S(2)}) copy-start(bf16[1,2048,768]{2,1,0:T(8,128)(2,1)} %param.18) | copy-start | bytes 9437188
  14.4 136.8 %copy-start.2 = (bf16[1,768,2048]{2,1,0:T(8,128)(2,1)S(1)}, bf16[1,768,2048]{2,1,0:T(8,128)(2,1)}, u32[]{:S(2)}) copy-start(bf16[1,768,2048]{2,1,0:T(8,128)(2,1)} %param.19) | copy-start | bytes 9437188
  175.5 73.3 %copy-start.4 = (bf16[128,2048]{1,0:T(8,128)(2,1)S(1)}, bf16[128,2048]{1,0:T(8,128)(2,1)}, u32[]{:S(2)}) copy-start(bf16[128,2048]{1,0:T(8,128)(2,1)} %grad_ref.2) | copy-start | bytes 1572868
  175.5 73.3 %copy-start.5 = (bf16[128,2048]{1,0:T(8,128)(2,1)S(1)}, bf16[128,2048]{1,0:T(8,128)(2,1)}, u32[]{:S(2)}) copy-start(bf16[128,2048]{1,0:T(8,128)(2,1)} %hid_ref.2) | copy-start | bytes 1572868
  175.5 73.3 %copy-start.6 = (f32[2048]{0:T(1024)S(1)}, f32[2048]{0:T(1024)}, u32[]{:S(2)}) copy-start(f32[2048]{0:T(1024)} %param.14) | copy-start | bytes 24580
  175.5 73.2 %all-to-all-start.1 = ((bf16[128,8,2688]{2,1,0:T(8,128)(2,1)}), bf16[128,8,2688]{2,1,0:T(8,128)(2,1)}, u32[]{:S(2)}, u32[]{:S(2)}) async-start(bf16[128,8,2688]{2,1,0:T(8,128)(2,1)} %bitcast.23), calls=%async_computation.1 | async-start | bytes 11010048 | tf_op jit(solution)/shard_map/all_to_all | solution.py:573
  183.6 1.3 copy-start.3
  261.8 21.7 %all-to-all-start.2 = ((bf16[16,256,128]{2,1,0:T(8,128)(2,1)}), bf16[16,256,128]{2,1,0:T(8,128)(2,1)S(1)}, u32[]{:S(2)}, u32[]{:S(2)}) async-start(bf16[16,256,128]{2,1,0:T(8,128)(2,1)} %bitcast.12), calls=%async_computation.2 | async-start | bytes 2097152 | tf_op jit(solution)/shard_map/all_to_all | solution.py:623
Sparse Core Ops, SparseCore 0:
  11.7 177.3 all-gather.2
